TPU v7x, 512 devices: a whole 4x8x8 slice. The times are simulated.
512 devices in a mesh: group: 8 (over y), mesh: 32 (over z, x), comp: 2 (over core).
Axes of the slice: x: 4, y: 8, z: 8, core: 2. Of those that a mesh axis runs over, the one named last changes fastest.
Arguments:
- log_sigma: float32 [2048, 128], P('mesh'), may hold values from -1 to 1
- block_owner: int32 [8, 4096, 1], P('group', 'mesh'), may hold values from 0 to 31; in each aligned block of 128 rows (0 to 127, 128 to 255, ..., all dimensions but the last counted through in order) at most 8 rows name the same one
- block_slot: int32 [8, 4096], P('group', 'mesh'), may hold values from 0 to 63
- coupling: float32 [128, 128], replicated, may hold values from -0.6 to 10, as said below
- sources: float32 [8, 2, 8, 4096, 128], P('group', 'comp', None, 'mesh'), may hold values from -24 to 24
- rcv_cell: int32 [8, 4096], P('group', 'mesh'), may hold values from 0 to 16383
- observed: float32 [8, 2, 8, 4096], P('group', 'comp', None, 'mesh'), may hold values from -6 to 6
Outputs:
- gradient: float32 [2048, 128], P('mesh')
Inputs may be any that keep to these rules, and one draw needn't show every extreme that they name: `block_owner`: in the 128 rows of one device of a group, no owner is named more than 8 times; some owner is named exactly 8 times in some device's rows. `rcv_cell`: A receiver's cell counts from the first cell of the modelling section of the device that holds the receiver's entry. `coupling`: every diagonal entry is 6 or more.
All inputs are finite; a program needn't handle non-finite values.
Results may differ from a plain program's by a relative error of at most 0.0003.
Values sent between devices are 32-bit elements; how exact they have to be, the bound alone decides.
A program may use at most 64 MiB of HBM per device.

v0:
```python
import jax
import jax.numpy as jnp
from jax import lax
from jax.sharding import PartitionSpec as P

CELLS = 128
S = 8
ITERS = 6


omega_freq = 0.8
chain_weight = 1.0


def from_partner(value, axis, distance):
    mask = 2**distance
    pairs = [(source, source ^ mask) for source in range(lax.axis_size(axis))]
    return lax.ppermute(value, axis, pairs)


def with_halo(x, sides, width):
    for axis, dim in sides:
        size, length = (lax.axis_size(axis), x.shape[dim])
        up = [(i, (i + 1) % size) for i in range(size - 1)]
        down = [(j, i) for i, j in up]
        last = lax.slice_in_dim(x, length - width, length, axis=dim)
        initial = lax.slice_in_dim(x, 0, width, axis=dim)
        before = lax.ppermute(last, axis, up)
        after = lax.ppermute(initial, axis, down)
        x = jnp.concatenate([before, x, after], axis=dim)
    return x


def partner(values):
    return from_partner(values, "comp", 0)


def beside(values):
    padded = with_halo(values, (("mesh", 1),), 1)
    return padded[:, :-2] + padded[:, 2:]


def cell_product(values, matrix):
    shaped = values.reshape(values.shape[:-1] + (-1, CELLS))
    product = jnp.einsum("...bj,ij->...bi", shaped, matrix, precision=lax.Precision.HIGHEST)
    return product.reshape(values.shape)


def operate(values, matrix, cross_coef):
    return (
        cell_product(values, matrix) - chain_weight * beside(values) + cross_coef * partner(values)
    )


def relax(right, matrix, cross_coef, inverse_diag, apply_op):
    state = jnp.zeros_like(right)
    for iteration in range(ITERS):
        state = state + inverse_diag * (right - apply_op(state, matrix, cross_coef))
    return state


def local(log_sigma, block_owner, block_slot, coupling, sources, rcv_cell, observed):
    owners = block_owner[0, :, 0]
    slots = block_slot[0]
    blocks_dev = owners.shape[0]
    inv_rows = log_sigma.shape[0]
    targets = owners * inv_rows + slots
    gathered = lax.all_gather(log_sigma, "mesh", axis=0, tiled=True)
    model_part = jnp.take(gathered, targets, axis=0)
    sigmas = jnp.exp(model_part).reshape(-1)
    receivers = rcv_cell[0]
    parity = (2 * lax.axis_index("comp") - 1).astype(jnp.float32)
    forward_coef = parity * omega_freq * sigmas
    inverse_diag = jnp.tile(1.0 / jnp.diagonal(coupling), blocks_dev)
    right = sources.reshape(S, -1)
    field_now = relax(right, coupling, forward_coef, inverse_diag, operate)
    field_other = partner(field_now)
    misfit = field_now[:, receivers] - observed[0, 0]
    adjoint_src = jnp.zeros_like(right).at[:, receivers].add(misfit)
    adjoint = relax(adjoint_src, coupling.T, -forward_coef, inverse_diag, operate)
    weighted = -parity * jnp.sum(adjoint * field_other, axis=0)
    partial_rows = (omega_freq * sigmas * weighted).reshape(blocks_dev, CELLS)
    inside_rows = (targets >= 0) & (targets < inv_rows * lax.axis_size("mesh"))
    kept_rows = jnp.where(inside_rows, targets, inv_rows * lax.axis_size("mesh"))
    owned = lax.psum_scatter(
        jnp.zeros((inv_rows * lax.axis_size("mesh"), CELLS), jnp.float32)
        .at[kept_rows]
        .add(partial_rows, mode="drop"),
        "mesh",
        scatter_dimension=0,
        tiled=True,
    )
    return lax.psum(owned, ("group", "comp"))


def solution(mesh):
    in_specs = (
        P("mesh", None),
        P("group", "mesh", None),
        P("group", "mesh"),
        P(),
        P("group", "comp", None, "mesh", None),
        P("group", "mesh"),
        P("group", "comp", None, "mesh"),
    )
    out_specs = P("mesh", None)
    return jax.shard_map(local, mesh=mesh, in_specs=in_specs, out_specs=out_specs, check_vma=False)
```

profile of v0, /device:TPU:1, one launch (start us, length us, event | category | flops | bytes accessed | tf_op | source)
XLA Modules:
  0.0 530.6 jit_solution(2460921501740615536)
XLA Ops:
  7.3 1.3 collective-permute-start.1
  8.6 4.6 collective-permute-start
  13.3 8.8 %collective-permute-start.2 = (f32[8,16384]{1,0:T(8,128)S(1)}, f32[8,16384]{1,0:T(8,128)S(1)}, u32[]{:S(2)}, u32[]{:S(2)}) collective-permute-start(f32[8,16384]{1,0:T(8,128)S(1)} %broadcast.154.clone), channel_id=1, source_target_pairs={{0,1},{1,0},{2,3},{3,2},{4,5},{5,4},{6,7},{7,6},{8,9},{9,8},{10,11... | collective-permute-start | bytes 1572872 | tf_op jit(solution)/shard_map/ppermute | solution.py:18
  22.1 1.2 gather_fusion.1
  25.3 68.6 %all-gather.2.cloned.1.call-done = f32[2048,128]{1,0:T(8,128)} async-done(((f32[64,128]{1,0:T(8,128)}), f32[2048,128]{1,0:T(8,128)}) %all-gather.2.cloned.1.call-update) | async-done | bytes 1048592 | tf_op jit(solution)/shard_map/all_gather | solution.py:68
  93.9 1.9 gather_fusion
  95.9 1.7 fusion.8
  97.5 7.0 %collective-permute-start.5 = (f32[8,16384]{1,0:T(8,128)S(1)}, f32[8,16384]{1,0:T(8,128)S(1)}, u32[]{:S(2)}, u32[]{:S(2)}) collective-permute-start(f32[8,16384]{1,0:T(8,128)S(1)} %fusion.8), channel_id=1, source_target_pairs={{0,1},{1,0},{2,3},{3,2},{4,5},{5,4},{6,7},{7,6},{8,9},{9,8},{10,11... | collective-permute-start | bytes 1572872 | tf_op jit(solution)/shard_map/ppermute | solution.py:18
  104.6 1.3 collective-permute-start.4
  105.9 4.0 collective-permute-start.3
  109.9 0.7 collective-permute-done.3
  110.7 1.9 fusion.10
  112.6 3.1 collective-permute-start.8
  115.7 1.3 collective-permute-start.7
  117.0 4.5 collective-permute-start.6
  122.8 2.8 collective-permute-start.11
  125.7 1.3 collective-permute-start.10
  126.9 4.5 collective-permute-start.9
  132.2 0.9 fusion.14
  133.1 2.8 collective-permute-start.14
  136.0 1.3 collective-permute-start.13
  137.3 4.5 collective-permute-start.12
  143.1 2.8 collective-permute-start.17
  146.6 1.3 collective-permute-start.16
  147.9 5.2 collective-permute-start.15
  153.9 1.9 fusion.18
  155.8 5.3 %copy.271 = f32[8,16384]{0,1:T(8,128)} copy(f32[8,16384]{1,0:T(8,128)S(1)} %fusion.18) | data formatting | bytes 1048576 | tf_op jit(solution)/shard_map/add | solution.py:58
  161.1 5.9 %scatter_custom_fusion = f32[8,16384]{0,1:T(8,128)} fusion(s32[128]{0:T(128)S(1)} %fusion.122, f32[]{:T(128)} %constant.12.clone.1, f32[1,1,8,128]{2,3,1,0:T(8,128)S(1)} %copy.272, f32[8,16384]{0,1:T(8,128)} %copy.271, s32[1024]{0:T(1024)S(1)} %pad_clamp_fusion), kind=kCustom, calls=%fused_computation.15 | custom fusion | flops 2048 | bytes 1118212 | tf_op jit(solution)/shard_map/scatter-add | solution.py:79
  167.0 5.5 %copy.273 = f32[8,16384]{1,0:T(8,128)S(1)} copy(f32[8,16384]{0,1:T(8,128)} %scatter_custom_fusion) | data formatting | bytes 1048576 | tf_op jit(solution)/shard_map/scatter-add | solution.py:79
  173.0 2.8 collective-permute-start.20
  175.9 1.3 collective-permute-start.19
  177.2 6.7 %collective-permute-start.18 = (f32[8,1]{1,0:T(8,128)S(1)}, f32[8,1]{1,0:T(8,128)S(1)}, u32[]{:S(2)}, u32[]{:S(2)}) collective-permute-start(f32[8,1]{1,0:T(8,128)S(1)} %get-tuple-element.15), channel_id=1, source_target_pairs={{0,2},{2,4},{4,6},{6,8},{8,10},{10,12},{12,14},{14,16},{16,18},{18... | collective-permute-start | bytes 104 | tf_op jit(solution)/shard_map/ppermute | solution.py:28
  185.3 2.8 collective-permute-start.23
  188.1 1.3 collective-permute-start.22
  189.4 6.6 %collective-permute-start.21 = (f32[8,1]{1,0:T(8,128)S(1)}, f32[8,1]{1,0:T(8,128)S(1)}, u32[]{:S(2)}, u32[]{:S(2)}) collective-permute-start(f32[8,1]{1,0:T(8,128)S(1)} %get-tuple-element.13), channel_id=1, source_target_pairs={{0,2},{2,4},{4,6},{6,8},{8,10},{10,12},{12,14},{14,16},{16,18},{18... | collective-permute-start | bytes 104 | tf_op jit(solution)/shard_map/ppermute | solution.py:28
  197.2 2.8 collective-permute-start.26
  200.0 1.3 collective-permute-start.25
  201.3 6.7 %collective-permute-start.24 = (f32[8,1]{1,0:T(8,128)S(1)}, f32[8,1]{1,0:T(8,128)S(1)}, u32[]{:S(2)}, u32[]{:S(2)}) collective-permute-start(f32[8,1]{1,0:T(8,128)S(1)} %get-tuple-element.11), channel_id=1, source_target_pairs={{0,2},{2,4},{4,6},{6,8},{8,10},{10,12},{12,14},{14,16},{16,18},{18... | collective-permute-start | bytes 104 | tf_op jit(solution)/shard_map/ppermute | solution.py:28
  209.4 2.8 collective-permute-start.29
  212.2 1.9 collective-permute-start.33
  214.2 1.3 collective-permute-start.28
  215.5 6.6 %collective-permute-start.27 = (f32[8,1]{1,0:T(8,128)S(1)}, f32[8,1]{1,0:T(8,128)S(1)}, u32[]{:S(2)}, u32[]{:S(2)}) collective-permute-start(f32[8,1]{1,0:T(8,128)S(1)} %get-tuple-element.9), channel_id=1, source_target_pairs={{0,2},{2,4},{4,6},{6,8},{8,10},{10,12},{12,14},{14,16},{16,18},{18... | collective-permute-start | bytes 104 | tf_op jit(solution)/shard_map/ppermute | solution.py:28
  223.3 3.3 collective-permute-start.32
  226.6 1.3 collective-permute-start.31
  227.9 6.6 %collective-permute-start.30 = (f32[8,1]{1,0:T(8,128)S(1)}, f32[8,1]{1,0:T(8,128)S(1)}, u32[]{:S(2)}, u32[]{:S(2)}) collective-permute-start(f32[8,1]{1,0:T(8,128)S(1)} %get-tuple-element.7), channel_id=1, source_target_pairs={{0,2},{2,4},{4,6},{6,8},{8,10},{10,12},{12,14},{14,16},{16,18},{18... | collective-permute-start | bytes 104 | tf_op jit(solution)/shard_map/ppermute | solution.py:28
  235.7 2.1 scatter_custom_fusion.1
  237.8 237.3 %reduce-scatter.2.cloned.1.call-done = f32[64,128]{1,0:T(8,128)} async-done(((f32[2048,128]{1,0:T(8,128)}), f32[64,128]{1,0:T(8,128)}) %reduce-scatter.2.cloned.1.call-update) | async-done | bytes 32784 | tf_op jit(solution)/shard_map/reduce_scatter | solution.py:85
  475.2 48.6 %psum.7 = f32[64,128]{1,0:T(8,128)} all-reduce(f32[64,128]{1,0:T(8,128)} %reduce-scatter.2.cloned.1.call-done), channel_id=1, replica_groups=mesh['group'=8,'mesh'=32,'comp'=2] {'group','comp'}, use_global_device_ids=true, to_apply=%region_4.5 | all-reduce | flops 8192 | bytes 65536 | tf_op jit(solution)/shard_map/psum | solution.py:93
  (82 shorter events, 14.8 us)
Async XLA Ops:
  6.5 15.5 %copy-start = (f32[128,128]{1,0:T(8,128)S(1)}, f32[128,128]{1,0:T(8,128)}, u32[]{:S(2)}) copy-start(f32[128,128]{1,0:T(8,128)} %param.10) | copy-start | bytes 196612
  6.5 115.8 %copy-start.1 = (f32[1,1,8,128,128]{4,3,2,1,0:T(8,128)S(1)}, f32[1,1,8,128,128]{4,3,2,1,0:T(8,128)}, u32[]{:S(2)}) copy-start(f32[1,1,8,128,128]{4,3,2,1,0:T(8,128)} %param.11) | copy-start | bytes 1572868
  6.5 87.3 %all-gather.2.cloned.1.call-start = ((), (), s32[]{:S(2)}) async-start(), calls=%async_computation.1 | async-start | bytes 1081344 | tf_op jit(solution)/shard_map/all_gather | solution.py:68
  7.3 467.9 %reduce-scatter.2.cloned.1.call-start = ((), (), s32[]{:S(2)}) async-start(), calls=%async_computation.2 | async-start | bytes 1081344 | tf_op jit(solution)/shard_map/reduce_scatter | solution.py:85
  7.3 88.5 %collective-permute-start.1 = (f32[8,1]{1,0:T(8,128)S(1)}, f32[8,1]{1,0:T(8,128)S(1)}, u32[]{:S(2)}, u32[]{:S(2)}) collective-permute-start(f32[8,1]{1,0:T(8,128)S(1)} %broadcast.157), channel_id=1, source_target_pairs={{2,0},{4,2},{6,4},{8,6},{10,8},{12,10},{14,12},{16,14},{18,16},{20... | collective-permute-start | bytes 104 | tf_op jit(solution)/shard_map/ppermute | solution.py:29
  8.6 87.2 %collective-permute-start = (f32[8,1]{1,0:T(8,128)S(1)}, f32[8,1]{1,0:T(8,128)S(1)}, u32[]{:S(2)}, u32[]{:S(2)}) collective-permute-start(f32[8,1]{1,0:T(8,128)S(1)} %broadcast.157), channel_id=1, source_target_pairs={{0,2},{2,4},{4,6},{6,8},{8,10},{10,12},{12,14},{14,16},{16,18},{18... | collective-permute-start | bytes 104 | tf_op jit(solution)/shard_map/ppermute | solution.py:28
  13.2 132.6 %copy-start.3 = (s32[1,128]{1,0:T(1,128)S(1)}, s32[1,128]{1,0:T(1,128)}, u32[]{:S(2)}) copy-start(s32[1,128]{1,0:T(1,128)} %param.12) | copy-start | bytes 1540
  13.3 132.6 %copy-start.2 = (f32[1,1,8,128]{3,2,1,0:T(8,128)S(1)}, f32[1,1,8,128]{3,2,1,0:T(8,128)}, u32[]{:S(2)}) copy-start(f32[1,1,8,128]{3,2,1,0:T(8,128)} %param.13) | copy-start | bytes 12292
  13.3 82.6 %collective-permute-start.2 = (f32[8,16384]{1,0:T(8,128)S(1)}, f32[8,16384]{1,0:T(8,128)S(1)}, u32[]{:S(2)}, u32[]{:S(2)}) collective-permute-start(f32[8,16384]{1,0:T(8,128)S(1)} %broadcast.154.clone), channel_id=1, source_target_pairs={{0,1},{1,0},{2,3},{3,2},{4,5},{5,4},{6,7},{7,6},{8,9},{9,8},{10,11... | collective-permute-start | bytes 1572872 | tf_op jit(solution)/shard_map/ppermute | solution.py:18
  97.5 13.1 %collective-permute-start.5 = (f32[8,16384]{1,0:T(8,128)S(1)}, f32[8,16384]{1,0:T(8,128)S(1)}, u32[]{:S(2)}, u32[]{:S(2)}) collective-permute-start(f32[8,16384]{1,0:T(8,128)S(1)} %fusion.8), channel_id=1, source_target_pairs={{0,1},{1,0},{2,3},{3,2},{4,5},{5,4},{6,7},{7,6},{8,9},{9,8},{10,11... | collective-permute-start | bytes 1572872 | tf_op jit(solution)/shard_map/ppermute | solution.py:18
  104.6 5.3 collective-permute-start.4
  105.9 4.7 collective-permute-start.3
  112.6 9.7 %collective-permute-start.8 = (f32[8,16384]{1,0:T(8,128)S(1)}, f32[8,16384]{1,0:T(8,128)S(1)}, u32[]{:S(2)}, u32[]{:S(2)}) collective-permute-start(f32[8,16384]{1,0:T(8,128)S(1)} %fusion.10), channel_id=1, source_target_pairs={{0,1},{1,0},{2,3},{3,2},{4,5},{5,4},{6,7},{7,6},{8,9},{9,8},{10,11... | collective-permute-start | bytes 1572872 | tf_op jit(solution)/shard_map/ppermute | solution.py:18
  115.7 6.4 %collective-permute-start.7 = (f32[8,1]{1,0:T(8,128)S(1)}, f32[8,1]{1,0:T(8,128)S(1)}, u32[]{:S(2)}, u32[]{:S(2)}) collective-permute-start(f32[8,1]{1,0:T(8,128)S(1)} %get-tuple-element.24), channel_id=1, source_target_pairs={{2,0},{4,2},{6,4},{8,6},{10,8},{12,10},{14,12},{16,14},{18,16},{20... | collective-permute-start | bytes 104 | tf_op jit(solution)/shard_map/ppermute | solution.py:29
  117.0 5.3 collective-permute-start.6
  122.8 9.4 %collective-permute-start.11 = (f32[8,16384]{1,0:T(8,128)S(1)}, f32[8,16384]{1,0:T(8,128)S(1)}, u32[]{:S(2)}, u32[]{:S(2)}) collective-permute-start(f32[8,16384]{1,0:T(8,128)S(1)} %fusion.12), channel_id=1, source_target_pairs={{0,1},{1,0},{2,3},{3,2},{4,5},{5,4},{6,7},{7,6},{8,9},{9,8},{10,11... | collective-permute-start | bytes 1572872 | tf_op jit(solution)/shard_map/ppermute | solution.py:18
  125.7 5.8 %collective-permute-start.10 = (f32[8,1]{1,0:T(8,128)S(1)}, f32[8,1]{1,0:T(8,128)S(1)}, u32[]{:S(2)}, u32[]{:S(2)}) collective-permute-start(f32[8,1]{1,0:T(8,128)S(1)} %get-tuple-element.22), channel_id=1, source_target_pairs={{2,0},{4,2},{6,4},{8,6},{10,8},{12,10},{14,12},{16,14},{18,16},{20... | collective-permute-start | bytes 104 | tf_op jit(solution)/shard_map/ppermute | solution.py:29
  126.9 5.3 collective-permute-start.9
  133.1 9.4 %collective-permute-start.14 = (f32[8,16384]{1,0:T(8,128)S(1)}, f32[8,16384]{1,0:T(8,128)S(1)}, u32[]{:S(2)}, u32[]{:S(2)}) collective-permute-start(f32[8,16384]{1,0:T(8,128)S(1)} %fusion.14), channel_id=1, source_target_pairs={{0,1},{1,0},{2,3},{3,2},{4,5},{5,4},{6,7},{7,6},{8,9},{9,8},{10,11... | collective-permute-start | bytes 1572872 | tf_op jit(solution)/shard_map/ppermute | solution.py:18
  136.0 6.4 %collective-permute-start.13 = (f32[8,1]{1,0:T(8,128)S(1)}, f32[8,1]{1,0:T(8,128)S(1)}, u32[]{:S(2)}, u32[]{:S(2)}) collective-permute-start(f32[8,1]{1,0:T(8,128)S(1)} %get-tuple-element.20), channel_id=1, source_target_pairs={{2,0},{4,2},{6,4},{8,6},{10,8},{12,10},{14,12},{16,14},{18,16},{20... | collective-permute-start | bytes 104 | tf_op jit(solution)/shard_map/ppermute | solution.py:29
  137.3 5.3 collective-permute-start.12
  143.1 10.8 %collective-permute-start.17 = (f32[8,16384]{1,0:T(8,128)S(1)}, f32[8,16384]{1,0:T(8,128)}, u32[]{:S(2)}, u32[]{:S(2)}) collective-permute-start(f32[8,16384]{1,0:T(8,128)S(1)} %fusion.16), channel_id=1, source_target_pairs={{0,1},{1,0},{2,3},{3,2},{4,5},{5,4},{6,7},{7,6},{8,9},{9,8},{10,11... | collective-permute-start | bytes 1572872 | tf_op jit(solution)/shard_map/ppermute | solution.py:18
  146.6 6.5 %collective-permute-start.16 = (f32[8,1]{1,0:T(8,128)S(1)}, f32[8,1]{1,0:T(8,128)S(1)}, u32[]{:S(2)}, u32[]{:S(2)}) collective-permute-start(f32[8,1]{1,0:T(8,128)S(1)} %get-tuple-element.18), channel_id=1, source_target_pairs={{2,0},{4,2},{6,4},{8,6},{10,8},{12,10},{14,12},{16,14},{18,16},{20... | collective-permute-start | bytes 104 | tf_op jit(solution)/shard_map/ppermute | solution.py:29
  147.9 6.0 %collective-permute-start.15 = (f32[8,1]{1,0:T(8,128)S(1)}, f32[8,1]{1,0:T(8,128)S(1)}, u32[]{:S(2)}, u32[]{:S(2)}) collective-permute-start(f32[8,1]{1,0:T(8,128)S(1)} %get-tuple-element.17), channel_id=1, source_target_pairs={{0,2},{2,4},{4,6},{6,8},{8,10},{10,12},{12,14},{14,16},{16,18},{18... | collective-permute-start | bytes 104 | tf_op jit(solution)/shard_map/ppermute | solution.py:28
  173.0 11.6 %collective-permute-start.20 = (f32[8,16384]{1,0:T(8,128)S(1)}, f32[8,16384]{1,0:T(8,128)S(1)}, u32[]{:S(2)}, u32[]{:S(2)}) collective-permute-start(f32[8,16384]{1,0:T(8,128)S(1)} %fusion.5), channel_id=1, source_target_pairs={{0,1},{1,0},{2,3},{3,2},{4,5},{5,4},{6,7},{7,6},{8,9},{9,8},{10,11... | collective-permute-start | bytes 1572872 | tf_op jit(solution)/shard_map/ppermute | solution.py:18
  175.9 8.0 %collective-permute-start.19 = (f32[8,1]{1,0:T(8,128)S(1)}, f32[8,1]{1,0:T(8,128)S(1)}, u32[]{:S(2)}, u32[]{:S(2)}) collective-permute-start(f32[8,1]{1,0:T(8,128)S(1)} %get-tuple-element.16), channel_id=1, source_target_pairs={{2,0},{4,2},{6,4},{8,6},{10,8},{12,10},{14,12},{16,14},{18,16},{20... | collective-permute-start | bytes 104 | tf_op jit(solution)/shard_map/ppermute | solution.py:29
  177.2 7.4 %collective-permute-start.18 = (f32[8,1]{1,0:T(8,128)S(1)}, f32[8,1]{1,0:T(8,128)S(1)}, u32[]{:S(2)}, u32[]{:S(2)}) collective-permute-start(f32[8,1]{1,0:T(8,128)S(1)} %get-tuple-element.15), channel_id=1, source_target_pairs={{0,2},{2,4},{4,6},{6,8},{8,10},{10,12},{12,14},{14,16},{16,18},{18... | collective-permute-start | bytes 104 | tf_op jit(solution)/shard_map/ppermute | solution.py:28
  185.3 11.5 %collective-permute-start.23 = (f32[8,16384]{1,0:T(8,128)S(1)}, f32[8,16384]{1,0:T(8,128)S(1)}, u32[]{:S(2)}, u32[]{:S(2)}) collective-permute-start(f32[8,16384]{1,0:T(8,128)S(1)} %fusion.50), channel_id=1, source_target_pairs={{0,1},{1,0},{2,3},{3,2},{4,5},{5,4},{6,7},{7,6},{8,9},{9,8},{10,11... | collective-permute-start | bytes 1572872 | tf_op jit(solution)/shard_map/ppermute | solution.py:18
  188.1 8.5 %collective-permute-start.22 = (f32[8,1]{1,0:T(8,128)S(1)}, f32[8,1]{1,0:T(8,128)S(1)}, u32[]{:S(2)}, u32[]{:S(2)}) collective-permute-start(f32[8,1]{1,0:T(8,128)S(1)} %get-tuple-element.14), channel_id=1, source_target_pairs={{2,0},{4,2},{6,4},{8,6},{10,8},{12,10},{14,12},{16,14},{18,16},{20... | collective-permute-start | bytes 104 | tf_op jit(solution)/shard_map/ppermute | solution.py:29
  189.4 7.4 %collective-permute-start.21 = (f32[8,1]{1,0:T(8,128)S(1)}, f32[8,1]{1,0:T(8,128)S(1)}, u32[]{:S(2)}, u32[]{:S(2)}) collective-permute-start(f32[8,1]{1,0:T(8,128)S(1)} %get-tuple-element.13), channel_id=1, source_target_pairs={{0,2},{2,4},{4,6},{6,8},{8,10},{10,12},{12,14},{14,16},{16,18},{18... | collective-permute-start | bytes 104 | tf_op jit(solution)/shard_map/ppermute | solution.py:28
  197.2 11.5 %collective-permute-start.26 = (f32[8,16384]{1,0:T(8,128)S(1)}, f32[8,16384]{1,0:T(8,128)S(1)}, u32[]{:S(2)}, u32[]{:S(2)}) collective-permute-start(f32[8,16384]{1,0:T(8,128)S(1)} %fusion.44), channel_id=1, source_target_pairs={{0,1},{1,0},{2,3},{3,2},{4,5},{5,4},{6,7},{7,6},{8,9},{9,8},{10,11... | collective-permute-start | bytes 1572872 | tf_op jit(solution)/shard_map/ppermute | solution.py:18
  200.0 8.0 %collective-permute-start.25 = (f32[8,1]{1,0:T(8,128)S(1)}, f32[8,1]{1,0:T(8,128)S(1)}, u32[]{:S(2)}, u32[]{:S(2)}) collective-permute-start(f32[8,1]{1,0:T(8,128)S(1)} %get-tuple-element.12), channel_id=1, source_target_pairs={{2,0},{4,2},{6,4},{8,6},{10,8},{12,10},{14,12},{16,14},{18,16},{20... | collective-permute-start | bytes 104 | tf_op jit(solution)/shard_map/ppermute | solution.py:29
  201.3 7.4 %collective-permute-start.24 = (f32[8,1]{1,0:T(8,128)S(1)}, f32[8,1]{1,0:T(8,128)S(1)}, u32[]{:S(2)}, u32[]{:S(2)}) collective-permute-start(f32[8,1]{1,0:T(8,128)S(1)} %get-tuple-element.11), channel_id=1, source_target_pairs={{0,2},{2,4},{4,6},{6,8},{8,10},{10,12},{12,14},{14,16},{16,18},{18... | collective-permute-start | bytes 104 | tf_op jit(solution)/shard_map/ppermute | solution.py:28
  209.4 13.4 %collective-permute-start.29 = (f32[8,16384]{1,0:T(8,128)S(1)}, f32[8,16384]{1,0:T(8,128)S(1)}, u32[]{:S(2)}, u32[]{:S(2)}) collective-permute-start(f32[8,16384]{1,0:T(8,128)S(1)} %fusion.38), channel_id=1, source_target_pairs={{0,1},{1,0},{2,3},{3,2},{4,5},{5,4},{6,7},{7,6},{8,9},{9,8},{10,11... | collective-permute-start | bytes 1572872 | tf_op jit(solution)/shard_map/ppermute | solution.py:18
  212.2 22.9 %collective-permute-start.33 = (f32[8,16384]{1,0:T(8,128)S(1)}, f32[8,16384]{1,0:T(8,128)S(1)}, u32[]{:S(2)}, u32[]{:S(2)}) collective-permute-start(f32[8,16384]{1,0:T(8,128)S(1)} %fusion.18), channel_id=1, source_target_pairs={{0,1},{1,0},{2,3},{3,2},{4,5},{5,4},{6,7},{7,6},{8,9},{9,8},{10,11... | collective-permute-start | bytes 1572872 | tf_op jit(solution)/shard_map/ppermute | solution.py:18
  214.2 8.5 %collective-permute-start.28 = (f32[8,1]{1,0:T(8,128)S(1)}, f32[8,1]{1,0:T(8,128)S(1)}, u32[]{:S(2)}, u32[]{:S(2)}) collective-permute-start(f32[8,1]{1,0:T(8,128)S(1)} %get-tuple-element.10), channel_id=1, source_target_pairs={{2,0},{4,2},{6,4},{8,6},{10,8},{12,10},{14,12},{16,14},{18,16},{20... | collective-permute-start | bytes 104 | tf_op jit(solution)/shard_map/ppermute | solution.py:29
  215.5 7.4 %collective-permute-start.27 = (f32[8,1]{1,0:T(8,128)S(1)}, f32[8,1]{1,0:T(8,128)S(1)}, u32[]{:S(2)}, u32[]{:S(2)}) collective-permute-start(f32[8,1]{1,0:T(8,128)S(1)} %get-tuple-element.9), channel_id=1, source_target_pairs={{0,2},{2,4},{4,6},{6,8},{8,10},{10,12},{12,14},{14,16},{16,18},{18... | collective-permute-start | bytes 104 | tf_op jit(solution)/shard_map/ppermute | solution.py:28
  223.3 12.0 %collective-permute-start.32 = (f32[8,16384]{1,0:T(8,128)S(1)}, f32[8,16384]{1,0:T(8,128)S(1)}, u32[]{:S(2)}, u32[]{:S(2)}) collective-permute-start(f32[8,16384]{1,0:T(8,128)S(1)} %fusion.32), channel_id=1, source_target_pairs={{0,1},{1,0},{2,3},{3,2},{4,5},{5,4},{6,7},{7,6},{8,9},{9,8},{10,11... | collective-permute-start | bytes 1572872 | tf_op jit(solution)/shard_map/ppermute | solution.py:18
  226.6 8.5 %collective-permute-start.31 = (f32[8,1]{1,0:T(8,128)S(1)}, f32[8,1]{1,0:T(8,128)S(1)}, u32[]{:S(2)}, u32[]{:S(2)}) collective-permute-start(f32[8,1]{1,0:T(8,128)S(1)} %get-tuple-element.8), channel_id=1, source_target_pairs={{2,0},{4,2},{6,4},{8,6},{10,8},{12,10},{14,12},{16,14},{18,16},{20... | collective-permute-start | bytes 104 | tf_op jit(solution)/shard_map/ppermute | solution.py:29
  227.9 7.4 %collective-permute-start.30 = (f32[8,1]{1,0:T(8,128)S(1)}, f32[8,1]{1,0:T(8,128)S(1)}, u32[]{:S(2)}, u32[]{:S(2)}) collective-permute-start(f32[8,1]{1,0:T(8,128)S(1)} %get-tuple-element.7), channel_id=1, source_target_pairs={{0,2},{2,4},{4,6},{6,8},{8,10},{10,12},{12,14},{14,16},{16,18},{18... | collective-permute-start | bytes 104 | tf_op jit(solution)/shard_map/ppermute | solution.py:28
Sparse Core Ops, SparseCore 0:
  10.5 83.2 all-gather.1
  238.0 237.1 reduce-scatter.1
where the time goes:
time: 534 us; the launch traced here: 531 us
  waiting for transfers between devices  311 us (58%)
  starting transfers between devices  118 us (22%)
  blocking collectives  48.6 us (9%)
  local copies, waits for them, and re-layouts  14.9 us (3%)
  between operations  14 us (3%)
  other arithmetic  13.8 us (3%)
  matrix products  10.1 us (2%)
    reduce_scatter x1, waiting for transfers between devices, local(): lax.psum_scatter(jnp.zeros((inv_rows * lax.axis_size('mesh'), CELLS), jnp...  237 us
    all_gather x1, waiting for transfers between devices, local(): gathered = lax.all_gather(log_sigma, 'mesh', axis=0, tiled=True)  68.6 us
    ppermute x11, starting transfers between devices, with_halo(): before = lax.ppermute(last, axis, up)  60.6 us
    psum x1, blocking collectives, local(): return lax.psum(owned, ('group', 'comp'))  48.6 us
    ppermute x12, starting transfers between devices, from_partner(): return lax.ppermute(value, axis, pairs)  43.4 us
    ppermute x11, starting transfers between devices, with_halo(): after = lax.ppermute(initial, axis, down)  14.1 us
  transfers between devices with their start and end apart: 36, of which 12 were waited for; matrix products, arithmetic and copies ran while one was open for 2% of the time, Pallas kernels for 0%

commit v1 on v0

v1 whole, which is shorter than its diff:
```python
import functools

import jax
import jax.numpy as jnp
from jax import lax
from jax.experimental import pallas as pl
from jax.experimental.pallas import tpu as pltpu
from jax.sharding import PartitionSpec as P

CELLS = 128
S = 8
ITERS = 6
CAP = 8
NX = 4
BLOCKS = 128
HALO = 8
HALF = (BLOCKS + 2 * HALO) // 2
ROWS = HALF * 8
STAGE = BLOCKS + 2 * HALO
OWNED = 64
OMEGA = 0.8
CHAIN = 1.0

f32, bf16, i32 = jnp.float32, jnp.bfloat16, jnp.int32
NT = (((1,), (1,)), ((), ()))


def iota(shape, dim):
    return lax.broadcasted_iota(i32, shape, dim)


def two(x):
    hi = x.astype(bf16)
    return hi, (x - hi.astype(f32)).astype(bf16)


def three(x):
    hi = x.astype(bf16)
    rest = x - hi.astype(f32)
    mid = rest.astype(bf16)
    return hi, mid, (rest - mid.astype(f32)).astype(bf16)


def dot(a, b):
    return jnp.dot(a, b, preferred_element_type=f32)


def dot_t(a, b):
    return lax.dot_general(a, b, NT, preferred_element_type=f32)


def column(row):
    n = row.shape[1]
    return jnp.sum(jnp.where(iota((n, n), 0) == iota((n, n), 1), row, 0.0), axis=1, keepdims=True)


def kernel(
    ng, nm, t_ref, rcv_ref, obs_ref, cpl_ref, ls_ref, src_ref, out_ref,
    stage, table, tn, rn, obs_own, obs_near, index_v, index_s, picked, theirs, choose,
    x_buf, lhs, mm, q, cross, wsig, hits, heard, count, wf, wa, qmat, psum_buf, part,
    slots, slots_in, pack, pack_in, grad, grad_in, line, total, total_in,
    local_sem, ex_send, ex_recv, halo_send, halo_recv, small_send, small_recv,
    ag_send, ag_recv, fan_send, pick_send, pick_recv, sl_send, sl_recv, gp_send, gp_recv,
    gr_send, gr_recv, ln_send, ln_recv, to_send, to_recv, index_sem,
):
    me = lax.axis_index("mesh")
    core = lax.axis_index("comp")
    grp = lax.axis_index("group")
    other = 1 - core
    nz = nm // NX
    mz, mx = me // NX, me % NX
    right, left = (me + 1) % nm, (me + nm - 1) % nm

    def far_first(i, n):
        return (n // 2 + ((i + 1) // 2) * (1 - 2 * (i % 2)) + n) % n

    def mesh_at(i):
        dz, dx = far_first(i // NX, nz), far_first(i % NX, NX)
        return ((mz + dz) % nz) * NX + (mx + dx) % NX

    def remote(src, dst, ssem, rsem, **where):
        return pltpu.make_async_remote_copy(
            src_ref=src, dst_ref=dst, send_sem=ssem, recv_sem=rsem,
            device_id=where, device_id_type=pl.DeviceIdType.MESH,
        )

    barrier = pltpu.get_barrier_semaphore()

    def greet(**where):
        pl.semaphore_signal(barrier, inc=1, device_id=where, device_id_type=pl.DeviceIdType.MESH)

    @pl.loop(0, nm - 1)
    def _(i):
        greet(mesh=mesh_at(i))

    @pl.loop(1, ng)
    def _(d):
        greet(group=(grp + d) % ng)

    greet(comp=other)
    greet(mesh=left, comp=other)
    greet(mesh=right, comp=other)

    own_half = pl.ds(pl.multiple_of(core * (OWNED // 2), 8), OWNED // 2)
    half_rows = OWNED // 2

    def table_rows(owner):
        return table.at[pl.ds(pl.multiple_of(owner * half_rows, 8), half_rows), :]

    own_table = pltpu.make_async_copy(ls_ref.at[own_half, :], table_rows(me), local_sem.at[4])
    own_table.start()

    def stage_rows(p, s, first, n):
        return stage.at[pl.ds(pl.multiple_of(p * (4 * STAGE) + s * STAGE + first, 8), n), :]

    def own_copy(s):
        return pltpu.make_async_copy(
            src_ref.at[4 * core + s], stage_rows(core, s, HALO, BLOCKS), local_sem.at[s]
        )

    @pl.loop(0, 4)
    def _(s):
        own_copy(s).start()

    eye = iota((CELLS, CELLS), 0) == iota((CELLS, CELLS), 1)
    beside = jnp.abs(iota((CELLS, CELLS), 0) - iota((CELLS, CELLS), 1)) == 1
    cpl = cpl_ref[...]
    dinv = 1.0 / jnp.sum(jnp.where(eye, cpl, 0.0), axis=0, keepdims=True)
    for m, w in ((cpl.T, wf), (cpl, wa)):
        scaled = -dinv * (jnp.where(eye, 0.0, m) - jnp.where(beside, CHAIN, 0.0))
        hi, lo = two(scaled)
        w[0:CELLS, 0:CELLS] = hi
        w[0:CELLS, CELLS:] = lo
        w[CELLS:, 0:CELLS] = hi
        w[CELLS:, CELLS:] = lo

    pl.semaphore_wait(barrier, nm - 1 + ng - 1 + 3)

    def along_z(i):
        z = (mz + far_first(i, nz)) % nz
        return remote(ls_ref.at[own_half, :], table_rows(me), ag_send.at[i], ag_recv.at[me], mesh=z * NX + mx)

    @pl.loop(0, nz - 1)
    def _(i):
        along_z(i).start()

    def small(k, **where):
        return (
            remote(t_ref, tn.at[k], small_send.at[k, 0], small_recv.at[k, 0], **where),
            remote(rcv_ref, rn.at[k], small_send.at[k, 1], small_recv.at[k, 1], **where),
        )

    smalls = small(0, mesh=right) + small(1, mesh=left)
    for c in smalls:
        c.start()

    def exchange(s):
        return remote(
            src_ref.at[4 * other + s], stage_rows(core, s, HALO, BLOCKS), ex_send.at[s], ex_recv.at[s], comp=other
        )

    @pl.loop(0, 4)
    def _(s):
        exchange(s).start()

    def halo(side, c, s):
        first, into = (BLOCKS - HALO, 0) if side == 0 else (0, STAGE - HALO)
        return remote(
            src_ref.at[4 * c + s, pl.ds(first, HALO), :], stage_rows(core, s, into, HALO),
            halo_send.at[side, c, s], halo_recv.at[side, core, s],
            mesh=right if side == 0 else left, comp=c,
        )

    @pl.loop(0, 8)
    def _(k):
        halo(0, k // 4, k % 4).start()
        halo(1, k // 4, k % 4).start()

    def obs_to(side, c):
        return remote(
            obs_ref, obs_near.at[side, core], halo_send.at[side, c, 4], halo_recv.at[side, core, 4],
            mesh=right if side == 0 else left, comp=c,
        )

    @pl.loop(0, 2)
    def _(c):
        obs_to(0, c).start()
        obs_to(1, c).start()

    obs_swap = remote(obs_ref, obs_own.at[core], ex_send.at[4], ex_recv.at[4], comp=other)
    obs_swap.start()
    obs_own[core] = obs_ref[...]

    t_row = t_ref[...]
    t_col = column(t_row.astype(f32))
    owner_row = t_row >> 6
    owner_col = t_col.astype(i32) >> 6
    earlier = (owner_col == owner_row) & (iota((BLOCKS, BLOCKS), 0) < iota((BLOCKS, BLOCKS), 1))
    rank = jnp.sum(jnp.where(earlier, 1.0, 0.0), axis=0, keepdims=True).astype(i32)
    place = owner_row * CAP + rank
    pick = jnp.where(iota((nm * CAP, BLOCKS), 0) == place, 1.0, 0.0)
    qmat[...] = pick.astype(bf16)
    slot_row = ((t_row & (OWNED - 1)) + 1).astype(f32)
    slot_of = jnp.sum(pick * slot_row, axis=1, keepdims=True)
    slots[...] = jnp.broadcast_to(slot_of, (nm * CAP, CELLS)).reshape(nm, CAP, CELLS)

    def along_x(i, k):
        z = (mz + far_first(nz - 1 - i, nz)) % nz
        owner = z * NX + mx
        return remote(
            table_rows(owner), table_rows(owner), fan_send.at[i, k], ag_recv.at[owner],
            mesh=mz * NX + (mx + far_first(k, NX)) % NX,
        )

    def arrived(owner):
        return remote(table_rows(owner), table_rows(owner), ag_send.at[0], ag_recv.at[owner], mesh=right)

    own_table.wait()

    @pl.loop(0, nz)
    def _(i):
        z = (mz + far_first(nz - 1 - i, nz)) % nz

        @pl.when(i > 0)
        def _():
            arrived(z * NX + mx).wait_recv()

        @pl.loop(0, NX - 1)
        def _(k):
            along_x(i, k).start()

    def tell(i):
        m = mesh_at(i)
        return remote(slots.at[m], slots_in.at[me], sl_send.at[m], sl_recv.at[me], mesh=m)

    @pl.loop(0, nm - 1)
    def _(i):
        tell(i).start()

    for c in smalls:
        c.wait_recv()
    near_l, near_r = tn[0], tn[1]
    index = jnp.concatenate([near_l, t_row, near_r] + [t_row] * 5, axis=0)
    index_v[...] = (index >> 6) * half_rows + (index & (half_rows - 1))
    to_scalars = pltpu.make_async_copy(index_v, index_s, index_sem)
    to_scalars.start()

    mine_row = jnp.where(((t_row >> 5) & 1) == core, 1.0, 0.0)
    mine_l = jnp.where(((near_l >> 5) & 1) == core, 1.0, 0.0)
    mine_r = jnp.where(((near_r >> 5) & 1) == core, 1.0, 0.0)
    wide = (HALO, BLOCKS)
    col_l = jnp.sum(jnp.where(iota(wide, 0) + BLOCKS - HALO == iota(wide, 1), mine_l, 0.0), axis=1, keepdims=True)
    col_r = jnp.sum(jnp.where(iota(wide, 0) == iota(wide, 1), mine_r, 0.0), axis=1, keepdims=True)
    choose[0:HALO, :] = jnp.broadcast_to(col_l, (HALO, CELLS))
    choose[HALO:HALO + BLOCKS, :] = jnp.broadcast_to(column(mine_row), (BLOCKS, CELLS))
    choose[HALO + BLOCKS:, :] = jnp.broadcast_to(col_r, (HALO, CELLS))

    obs_swap.wait_recv()
    for side in range(2):
        for p in range(2):
            remote(obs_ref, obs_near.at[side, p], halo_send.at[side, p, 4], halo_recv.at[side, p, 4], comp=other).wait_recv()

    odd = iota((8, CELLS), 0) % 2

    def receivers(cells, base, obs_at):
        block = (cells >> 7) + base - HALF * odd
        lane = jnp.where(iota((CELLS, CELLS), 0) == (cells & (CELLS - 1)), 1.0, 0.0).astype(bf16)
        values = []
        for p in range(2):
            rows = [obs_at[p, pl.ds(4 * core + s, 1), :] for s in range(4)]
            values.append(jnp.concatenate([rows[r // 2] for r in range(8)], axis=0))
        return block, lane, values

    def scatter(block, lane, values, i):
        at = jnp.tile(block, (8, 1)) == 8 * i + (iota((64, CELLS), 0) >> 3)
        twice = jnp.concatenate([lane, lane], axis=1)
        res = []
        for v in values:
            hi, lo = two(jnp.where(at, jnp.tile(v, (8, 1)), 0.0))
            res.append(dot_t(jnp.concatenate([hi, lo], axis=1), twice))
        return res, dot_t(jnp.where(at, 1.0, 0.0).astype(bf16), lane)

    here = receivers(rcv_ref[...], HALO, obs_own)

    @pl.loop(0, HALF // 8)
    def _(i):
        res, cnt = scatter(*here, i)
        rows = pl.ds(pl.multiple_of(64 * i, 64), 64)
        heard[0, rows, :] = res[0]
        heard[1, rows, :] = res[1]
        count[rows, :] = cnt

    for side, (base, i) in enumerate(((HALO - BLOCKS, 0), (HALO + BLOCKS, HALF // 8 - 1))):
        res, cnt = scatter(*receivers(rn[side], base, obs_near.at[side]), i)
        rows = slice(64 * i, 64 * i + 64)
        heard[0, rows, :] += res[0]
        heard[1, rows, :] += res[1]
        count[rows, :] += cnt

    @pl.loop(0, 4)
    def _(s):
        own_copy(s).wait()
        exchange(s).wait_recv()

    @pl.loop(0, 8)
    def _(k):
        for side in range(2):
            remote(
                src_ref.at[0, pl.ds(0, HALO), :], stage_rows(k // 4, k % 4, 0 if side == 0 else STAGE - HALO, HALO),
                halo_send.at[side, k // 4, k % 4], halo_recv.at[side, k // 4, k % 4], comp=other,
            ).wait_recv()

    even_rows = iota((64, CELLS), 0) % 2 == 0
    keep_l = jnp.where(even_rows & (me == 0), 0.0, 1.0)
    keep_r = jnp.where(jnp.logical_not(even_rows) & (me == nm - 1), 0.0, 1.0)

    def keep(i):
        return jnp.where(i == 0, keep_l, jnp.where(i == HALF // 8 - 1, keep_r, 1.0))

    def put(b, p, i, x):
        x_buf[b, p, pl.ds(pl.multiple_of(8 + 64 * i, 8), 64), :] = x
        hi, lo = two(x)
        rows = pl.ds(pl.multiple_of(p * ROWS + 64 * i, 64), 64)
        lhs[rows, 0:CELLS] = hi
        lhs[rows, CELLS:] = lo

    def seams(b):
        top = iota((8, CELLS), 0) % 2 == 0
        for p in range(2):
            end = x_buf[b, p, ROWS:ROWS + 8, :]
            start = x_buf[b, p, 8:16, :]
            x_buf[b, p, 0:8, :] = jnp.where(top, 0.0, pltpu.roll(end, 1, axis=0))
            x_buf[b, p, ROWS + 8:ROWS + 16, :] = jnp.where(top, pltpu.roll(start, 7, axis=0), 0.0)

    @pl.loop(0, HALF // 8)
    def _(i):
        mask = keep(i)
        for p in range(2):
            x = jnp.concatenate(
                [stage[pl.ds(p * (4 * STAGE) + 8 * i + j, 8, stride=HALF), :] for j in range(8)], axis=0
            )
            x = x * dinv * mask
            q[0, p, pl.ds(pl.multiple_of(64 * i, 64), 64), :] = x
            put(0, p, i, x)

    seams(0)

    @pl.loop(0, nz)
    def _(i):
        z = (mz + far_first(i, nz)) % nz

        @pl.loop(0, NX - 1)
        def _(k):
            arrived(z * NX + (mx + far_first(k, NX)) % NX).wait_recv()

    to_scalars.wait()

    def pick_rows(first, source, lane):
        picked[pl.ds(first, 8), :] = jnp.concatenate(
            [table[pl.ds(index_s[source, lane + j], 1), :] for j in range(8)], axis=0
        )

    pick_rows(0, 0, BLOCKS - HALO)
    pick_rows(HALO + BLOCKS, 2, 0)

    @pl.loop(0, BLOCKS // 8)
    def _(i):
        pick_rows(pl.multiple_of(HALO + 8 * i, 8), 1, 8 * i)

    swap = remote(picked, theirs, pick_send.at[0], pick_recv.at[0], comp=other)
    swap.start()
    swap.wait_recv()
    sigma = OMEGA * jnp.exp(jnp.where(choose[...] > 0.5, picked[...], theirs[...]))
    wsig[...] = sigma

    @pl.loop(0, HALF // 8)
    def _(i):
        mask = keep(i)
        rows = []
        for j in range(8):
            a = jnp.broadcast_to(wsig[pl.ds(8 * i + j, 1), :], (8, CELLS))
            b = jnp.broadcast_to(wsig[pl.ds(HALF + 8 * i + j, 1), :], (8, CELLS))
            rows.append(jnp.where(odd == 0, a, b))
        cross[pl.ds(pl.multiple_of(64 * i, 64), 64), :] = jnp.concatenate(rows, axis=0) * dinv * mask

    lane_row = iota((1, CELLS), 1)
    at_first = jnp.where(lane_row == 0, CHAIN * dinv, 0.0)
    at_last = jnp.where(lane_row == CELLS - 1, CHAIN * dinv, 0.0)

    def sweep(base, qk, sign, weights, step):
        old, new = base + step % 2, base + (step + 1) % 2
        mm[...] = dot(lhs[...], weights[...])

        @pl.loop(0, HALF // 8, unroll=True)
        def _(i):
            mask = keep(i)
            rows = pl.ds(pl.multiple_of(64 * i, 64), 64)
            turn = cross[rows, :]
            for p in range(2):
                prod = pl.ds(pl.multiple_of(p * ROWS + 64 * i, 64), 64)
                before = x_buf[old, p, pl.ds(pl.multiple_of(64 * i, 8), 64), :]
                after = x_buf[old, p, pl.ds(pl.multiple_of(64 * i + 16, 8), 64), :]
                across = x_buf[old, 1 - p, pl.ds(pl.multiple_of(64 * i + 8, 8), 64), :]
                x = q[qk, p, rows, :] + (mm[prod, 0:CELLS] + mm[prod, CELLS:])
                x = x + at_first * pltpu.roll(before, 1, axis=1) + at_last * pltpu.roll(after, CELLS - 1, axis=1)
                both = turn * across
                x = x + both if (sign > 0) == (p == 0) else x - both
                put(new, p, i, x * mask)

        seams(new)

    @pl.loop(0, ITERS - 1)
    def _(step):
        sweep(0, 0, 1, wf, step)

    fin = (ITERS - 1) % 2

    @pl.loop(0, HALF // 8)
    def _(i):
        mask = keep(i) * dinv
        rows = pl.ds(pl.multiple_of(64 * i, 64), 64)
        for p in range(2):
            field = x_buf[fin, p, pl.ds(pl.multiple_of(8 + 64 * i, 8), 64), :]
            x = mask * (count[rows, :] * field - heard[p, rows, :])
            q[1, p, rows, :] = x
            put(2, p, i, x)

    seams(2)

    @pl.loop(0, ITERS - 1)
    def _(step):
        sweep(2, 1, -1, wa, step)

    @pl.loop(0, HALF // 8)
    def _(i):
        rows = pl.ds(pl.multiple_of(8 + 64 * i, 8), 64)
        psum_buf[pl.ds(pl.multiple_of(64 * i, 64), 64), :] = (
            x_buf[2 + fin, 0, rows, :] * x_buf[fin, 1, rows, :]
            - x_buf[2 + fin, 1, rows, :] * x_buf[fin, 0, rows, :]
        )

    @pl.loop(0, BLOCKS // 16)
    def _(i):
        for h in range(2):
            first = 8 * (8 * i + (HALO if h == 0 else 0)) + h
            acc = psum_buf[pl.ds(first, 8, stride=8), :]
            for s in range(1, 4):
                acc = acc + psum_buf[pl.ds(first + 2 * s, 8, stride=8), :]
            at = 8 * i + (HALF - HALO) * h
            part[pl.ds(pl.multiple_of(at, 8), 8), :] = acc * wsig[pl.ds(pl.multiple_of(HALO + at, 8), 8), :]

    hi, mid, lo = three(part[...])
    sel = qmat[...]
    packed = dot(sel, hi) + dot(sel, mid) + dot(sel, lo)
    pack[...] = packed.reshape(nm, CAP, CELLS)

    def give(i):
        m = mesh_at(i)
        return remote(pack.at[m], pack_in.at[me], gp_send.at[m], gp_recv.at[me], mesh=m)

    @pl.loop(0, nm - 1)
    def _(i):
        give(i).start()

    pack_in[me] = pack[me]
    slots_in[me] = slots[me]

    @pl.loop(0, nm - 1)
    def _(i):
        m = mesh_at(i)
        remote(slots.at[m], slots_in.at[m], sl_send.at[m], sl_recv.at[m], mesh=m).wait_recv()

    slot_in = slots_in[...].reshape(nm * CAP, CELLS)
    hit = jnp.where(slot_in == (iota((nm * CAP, CELLS), 1) + 1).astype(f32), 1.0, 0.0)
    hits[...] = hit.T.astype(bf16)

    @pl.loop(0, nm - 1)
    def _(i):
        m = mesh_at(i)
        remote(pack.at[m], pack_in.at[m], gp_send.at[m], gp_recv.at[m], mesh=m).wait_recv()

    hi, mid, lo = three(pack_in[...].reshape(nm * CAP, CELLS))
    sel = hits[0:OWNED, :]
    grad[...] = dot(sel, hi) + dot(sel, mid) + dot(sel, lo)

    def half_of(ref, c):
        return ref.at[pl.ds(pl.multiple_of(c * half_rows, 8), half_rows), :]

    cores = remote(half_of(grad, other), grad_in, gr_send.at[0], gr_recv.at[0], comp=other)
    cores.start()
    cores.wait_recv()
    line[grp] = grad[pl.ds(pl.multiple_of(core * half_rows, 8), half_rows), :] + grad_in[...]

    def over_y(d):
        return remote(line.at[grp], line.at[grp], ln_send.at[d], ln_recv.at[grp], group=(grp + far_first(d, ng)) % ng)

    @pl.loop(0, ng - 1)
    def _(d):
        over_y(d).start()

    @pl.loop(0, ng - 1)
    def _(d):
        g = (grp + far_first(d, ng)) % ng
        remote(line.at[g], line.at[g], ln_send.at[d], ln_recv.at[g], group=g).wait_recv()

    summed = line[0]
    for g in range(1, ng):
        summed = summed + line[g]
    total[...] = summed
    back = remote(total, total_in, to_send.at[0], to_recv.at[0], comp=other)
    back.start()
    out_ref[pl.ds(pl.multiple_of(core * half_rows, 8), half_rows), :] = summed
    back.wait_recv()
    out_ref[pl.ds(pl.multiple_of(other * half_rows, 8), half_rows), :] = total_in[...]

    @pl.loop(0, nz - 1)
    def _(i):
        along_z(i).wait_send()

    for c in smalls:
        c.wait_send()

    @pl.loop(0, 4)
    def _(s):
        exchange(s).wait_send()

    @pl.loop(0, 8)
    def _(k):
        halo(0, k // 4, k % 4).wait_send()
        halo(1, k // 4, k % 4).wait_send()

    @pl.loop(0, 2)
    def _(c):
        obs_to(0, c).wait_send()
        obs_to(1, c).wait_send()

    obs_swap.wait_send()

    @pl.loop(0, nz)
    def _(i):
        @pl.loop(0, NX - 1)
        def _(k):
            along_x(i, k).wait_send()

    swap.wait_send()

    @pl.loop(0, nm - 1)
    def _(i):
        tell(i).wait_send()
        give(i).wait_send()

    cores.wait_send()

    @pl.loop(0, ng - 1)
    def _(d):
        over_y(d).wait_send()

    back.wait_send()


def local(log_sigma, block_owner, block_slot, coupling, sources, rcv_cell, observed):
    nm, ng = lax.axis_size("mesh"), lax.axis_size("group")
    targets = block_owner.reshape(1, BLOCKS) * OWNED + block_slot
    vmem, hbm, dma = pltpu.VMEM, pl.BlockSpec(memory_space=pl.ANY), pltpu.SemaphoreType.DMA
    inside = pl.BlockSpec(memory_space=pltpu.VMEM)
    nz = nm // NX
    return pl.pallas_call(
        functools.partial(kernel, ng, nm),
        out_shape=jax.ShapeDtypeStruct((OWNED, CELLS), f32),
        in_specs=[inside] * 4 + [hbm] * 2,
        out_specs=inside,
        scratch_shapes=[
            vmem((8 * STAGE, CELLS), f32),
            vmem((nm * OWNED // 2, CELLS), f32),
            vmem((2, 1, BLOCKS), i32),
            vmem((2, 1, BLOCKS), i32),
            vmem((2, S, CELLS), f32),
            vmem((2, 2, S, CELLS), f32),
            vmem((8, BLOCKS), i32),
            pltpu.SMEM((8, BLOCKS), i32),
            vmem((STAGE, CELLS), f32),
            vmem((STAGE, CELLS), f32),
            vmem((STAGE, CELLS), f32),
            vmem((4, 2, ROWS + 16, CELLS), f32),
            vmem((2 * ROWS, 2 * CELLS), bf16),
            vmem((2 * ROWS, 2 * CELLS), f32),
            vmem((2, 2, ROWS, CELLS), f32),
            vmem((ROWS, CELLS), f32),
            vmem((STAGE, CELLS), f32),
            vmem((CELLS, nm * CAP), bf16),
            vmem((2, ROWS, CELLS), f32),
            vmem((ROWS, CELLS), f32),
            vmem((2 * CELLS, 2 * CELLS), bf16),
            vmem((2 * CELLS, 2 * CELLS), bf16),
            vmem((nm * CAP, BLOCKS), bf16),
            vmem((ROWS, CELLS), f32),
            vmem((BLOCKS, CELLS), f32),
            vmem((nm, CAP, CELLS), f32),
            vmem((nm, CAP, CELLS), f32),
            vmem((nm, CAP, CELLS), f32),
            vmem((nm, CAP, CELLS), f32),
            vmem((OWNED, CELLS), f32),
            vmem((OWNED // 2, CELLS), f32),
            vmem((ng, OWNED // 2, CELLS), f32),
            vmem((OWNED // 2, CELLS), f32),
            vmem((OWNED // 2, CELLS), f32),
            dma((5,)),
            dma((5,)), dma((5,)),
            dma((2, 2, 5)), dma((2, 2, 5)),
            dma((2, 2)), dma((2, 2)),
            dma((nz,)), dma((nm,)), dma((nz, NX)),
            dma((1,)), dma((1,)),
            dma((nm,)), dma((nm,)),
            dma((nm,)), dma((nm,)),
            dma((1,)), dma((1,)),
            dma((ng,)), dma((ng,)),
            dma((1,)), dma((1,)),
            dma(()),
        ],
        compiler_params=pltpu.CompilerParams(collective_id=0, has_side_effects=True),
    )(
        targets, rcv_cell, observed.reshape(S, CELLS), coupling, log_sigma, sources.reshape(S, BLOCKS, CELLS)
    )


def solution(mesh):
    in_specs = (
        P("mesh", None),
        P("group", "mesh", None),
        P("group", "mesh"),
        P(),
        P("group", "comp", None, "mesh", None),
        P("group", "mesh"),
        P("group", "comp", None, "mesh"),
    )
    return jax.shard_map(local, mesh=mesh, in_specs=in_specs, out_specs=P("mesh", None), check_vma=False)
```

time: 534 us -> 61.9 us (0.12)
  waiting for transfers between devices: 311 us -> 0 us
  starting transfers between devices: 118 us -> 0 us
  Pallas kernels: 0 us -> 59.1 us
  blocking collectives: 48.6 us -> 0 us
  between operations: 14 us -> 0.01 us
  other arithmetic: 13.8 us -> 0.51 us
  local copies, waits for them, and re-layouts: 14.9 us -> 2.04 us
  matrix products: 10.1 us -> 0 us
    reduce_scatter x1 -> x0, waiting for transfers between devices: 237 us -> none  [local(): lax.psum_scatter(jnp.zeros((inv_rows * lax.axis_size('mesh'), CELLS), jnp...]
    ppermute x34 -> x0, starting transfers between devices: 118 us -> none  [the longest x11 60.6 us: with_halo(): before = lax.ppermute(last, axis, up)]
    all_gather x1 -> x0, waiting for transfers between devices: 68.6 us -> none  [local(): gathered = lax.all_gather(log_sigma, 'mesh', axis=0, tiled=True)]
    pallas_call x0 -> x1, Pallas kernels: none -> 59.1 us  [local(): pl.pallas_call(functools.partial(kernel, ng, nm), out_shape=jax.ShapeDtyp...]
    psum x1 -> x0, blocking collectives: 48.6 us -> none  [local(): return lax.psum(owned, ('group', 'comp'))]
    dot_general x12 -> x0, matrix products: 10.1 us -> none  [cell_product(): jnp.einsum('...bj,ij->...bi', shaped, matrix, precision=lax.Precision.HIG...]
    scatter-add x2 -> x0, other arithmetic: 8.05 us -> none  [the longest x1 5.95 us: local(): adjoint_src = jnp.zeros_like(right).at[:, receivers].add(misfit)]
    scatter-add x1 -> x0, local copies, waits for them, and re-layouts: 5.54 us -> none  [local(): adjoint_src = jnp.zeros_like(right).at[:, receivers].add(misfit)]
  transfers between devices with their start and end apart: 36 -> 0, of which waited for: 12 -> 0; matrix products, arithmetic and copies ran while one was open for 2% -> 0% of each run, Pallas kernels for 0% -> 0%
where the time goes in v1:
time: 61.9 us; the launch traced here: 61.7 us
  Pallas kernels  59.1 us (95%)
  local copies, waits for them, and re-layouts  2.04 us (3%)
    pallas_call x1, Pallas kernels, local(): pl.pallas_call(functools.partial(kernel, ng, nm), out_shape=jax.ShapeDtyp...  59.1 us
    unnamed x5, local copies, waits for them, and re-layouts  2.04 us

profile of v1, /device:TPU:1, one launch (start us, length us, event | category | flops | bytes accessed | tf_op | source)
XLA Modules:
  0.0 61.7 jit_solution(17500218892783999579)
XLA Ops:
  0.0 0.0 copy-start
  0.0 0.0 copy-start.1
  0.0 0.7 %copy-done = s32[1,128]{1,0:T(1,128)S(1)} copy-done((s32[1,128]{1,0:T(1,128)S(1)}, s32[1,128]{1,0:T(1,128)}, u32[]{:S(2)}) %copy-start) | copy-done | bytes 536
  0.7 0.0 copy-done.1
  0.7 0.5 bitcast_add_fusion.t_ref
  1.2 59.1 %shard_map.73 = f32[64,128]{1,0:T(8,128)} custom-call(s32[1,128]{1,0:T(1,128)} %bitcast_add_fusion.t_ref, s32[1,128]{1,0:T(1,128)} %rcv_ref.1, f32[8,128]{1,0:T(8,128)} %bitcast.5, f32[128,128]{1,0:T(8,128)} %cpl_ref.1, f32[64,128]{1,0:T(8,128)} %ls_ref.1, f32[8,128,128]{2,1,0:T(8,128)} %bitcast.4), custom_call_target="tpu_custom_call" | custom-call | tf_op jit(solution)/shard_map/pallas_call | solution.py:567
  60.3 1.4 %copy.9 = f32[64,128]{1,0:T(8,128)} copy(f32[64,128]{1,0:T(8,128)} %shard_map.73) | data formatting | bytes 65536
Async XLA Ops:
  0.0 0.7 %copy-start = (s32[1,128]{1,0:T(1,128)S(1)}, s32[1,128]{1,0:T(1,128)}, u32[]{:S(2)}) copy-start(s32[1,128]{1,0:T(1,128)} %param.9) | copy-start | bytes 1540
  0.0 0.7 %copy-start.1 = (s32[1,128,1]{1,2,0:T(1,128)S(1)}, s32[1,128,1]{1,2,0:T(1,128)}, u32[]{:S(2)}) copy-start(s32[1,128,1]{1,2,0:T(1,128)} %param.8) | copy-start | bytes 1540

commit v2 on v0

v2 whole, which is shorter than its diff:
```python
import functools

import jax
import jax.numpy as jnp
from jax import lax
from jax.experimental import pallas as pl
from jax.experimental.pallas import tpu as pltpu
from jax.sharding import PartitionSpec as P

CELLS = 128
S = 8
ITERS = 6
CAP = 8
NX = 4
BLOCKS = 128
HALO = 8
HALF = (BLOCKS + 2 * HALO) // 2
ROWS = HALF * 8
STAGE = BLOCKS + 2 * HALO
OWNED = 64
GROUP = 9
OMEGA = 0.8
CHAIN = 1.0

f32, bf16, i32 = jnp.float32, jnp.bfloat16, jnp.int32
NT = (((1,), (1,)), ((), ()))


def iota(shape, dim):
    return lax.broadcasted_iota(i32, shape, dim)


def two(x):
    hi = x.astype(bf16)
    return hi, (x - hi.astype(f32)).astype(bf16)


def three(x):
    hi = x.astype(bf16)
    rest = x - hi.astype(f32)
    mid = rest.astype(bf16)
    return hi, mid, (rest - mid.astype(f32)).astype(bf16)


def dot(a, b):
    return jnp.dot(a, b, preferred_element_type=f32)


def dot_t(a, b):
    return lax.dot_general(a, b, NT, preferred_element_type=f32)


def column(row):
    n = row.shape[1]
    return jnp.sum(jnp.where(iota((n, n), 0) == iota((n, n), 1), row, 0.0), axis=1, keepdims=True)


def kernel(
    ng, nm, own_ref, slot_ref, rcv_ref, obs_ref, cpl_ref, ls_ref, src_ref, out_ref,
    stage, table, near, obs_own, obs_near, index_v, index_s, picked, theirs, choose,
    fwd_a, fwd_b, adj_a, adj_b, lhs_hi, lhs_lo, q, cross, wsig, hits, heard, count, wf, wa, qmat, psum_buf, part,
    slots, slots_in, pack, pack_in, grad, grad_in, line, total, total_in,
    local_sem, ex_send, ex_recv, halo_send, halo_recv, obs_send, obs_recv, small_send, small_recv,
    ag_send, ag_recv, fan_send, fan_recv, pick_send, pick_recv, sl_send, sl_recv, gp_send, gp_recv,
    gr_send, gr_recv, ln_send, ln_recv, to_send, to_recv, index_sem,
):
    me = lax.axis_index("mesh")
    core = lax.axis_index("comp")
    grp = lax.axis_index("group")
    other = 1 - core
    nz = nm // NX
    mz, mx = lax.div(me, NX), lax.rem(me, NX)
    z_at = [lax.rem(mz + d, nz) * NX for d in range(nz)]
    x_at = [lax.rem(mx + d, NX) for d in range(NX)]
    g_at = [lax.rem(grp + d, ng) for d in range(ng)]
    right, left = lax.rem(me + 1, nm), lax.rem(me + nm - 1, nm)

    def ring(d, n):
        return min(d, n - d)

    far_z, far_x, far_g = (sorted(range(1, n), key=lambda d: -ring(d, n)) for n in (nz, NX, ng))
    far = sorted(
        [(z, x) for z in range(nz) for x in range(NX) if z or x], key=lambda d: -ring(d[0], nz) - ring(d[1], NX)
    )

    def remote(src, dst, ssem, rsem, g=None, m=None, c=None):
        where = (grp if g is None else g, me if m is None else m, core if c is None else c)
        return pltpu.make_async_remote_copy(
            src_ref=src, dst_ref=dst, send_sem=ssem, recv_sem=rsem,
            device_id=where, device_id_type=pl.DeviceIdType.MESH,
        )

    def bytes_of(ref, ssem, rsem):
        return remote(ref, ref, ssem, rsem, c=other)

    barrier = pltpu.get_barrier_semaphore()

    def greet(g=None, m=None, c=None):
        where = (grp if g is None else g, me if m is None else m, core if c is None else c)
        pl.semaphore_signal(barrier, inc=1, device_id=where, device_id_type=pl.DeviceIdType.MESH)

    for z, x in far:
        greet(m=z_at[z] + x_at[x])
    for d in far_g:
        greet(g=g_at[d])
    greet(m=left, c=other)
    greet(m=right, c=other)
    greet(c=other)

    half_rows = OWNED // 2
    own_half = pl.ds(pl.multiple_of(core * half_rows, 8), half_rows)

    def table_rows(owner):
        return table.at[pl.ds(pl.multiple_of(owner * half_rows, 8), half_rows), :]

    def stage_rows(p, s, first, n):
        return stage.at[pl.ds(pl.multiple_of(p * (4 * STAGE) + s * STAGE + first, 8), n), :]

    own_table = pltpu.make_async_copy(ls_ref.at[own_half, :], table_rows(me), local_sem.at[1])
    own_table.start()
    own_src = [
        pltpu.make_async_copy(src_ref.at[4 * core + s], stage_rows(core, s, HALO, BLOCKS), local_sem.at[s + 2])
        for s in range(4)
    ]
    for c in own_src:
        c.start()

    pl.semaphore_wait(barrier, nm - 1 + ng - 1 + 3)

    for z in far_z:
        remote(ls_ref.at[own_half, :], table_rows(me), ag_send.at[0], ag_recv.at[mz], m=z_at[z] + mx).start()

    for side, m in ((0, right), (1, left)):
        for k, ref in enumerate((own_ref, slot_ref, rcv_ref)):
            remote(ref, near.at[side, k], small_send.at[0], small_recv.at[0], m=m).start()
    for s in range(4):
        remote(
            src_ref.at[4 * other + s], stage_rows(core, s, HALO, BLOCKS), ex_send.at[0], ex_recv.at[0], c=other
        ).start()
    obs_swap = remote(obs_ref, obs_own.at[core], ex_send.at[1], ex_recv.at[1], c=other)
    obs_swap.start()
    for side, m, first, into in ((0, right, BLOCKS - HALO, 0), (1, left, 0, STAGE - HALO)):
        for c in range(2):
            for s in range(4):
                remote(
                    src_ref.at[4 * c + s, pl.ds(first, HALO), :], stage_rows(core, s, into, HALO),
                    halo_send.at[0], halo_recv.at[0], m=m, c=c,
                ).start()
            remote(obs_ref, obs_near.at[side, core], obs_send.at[0], obs_recv.at[0], m=m, c=c).start()
    obs_own[core] = obs_ref[...]

    eye = iota((CELLS, CELLS), 0) == iota((CELLS, CELLS), 1)
    beside = jnp.abs(iota((CELLS, CELLS), 0) - iota((CELLS, CELLS), 1)) == 1
    cpl = cpl_ref[...]
    dinv = 1.0 / jnp.sum(jnp.where(eye, cpl, 0.0), axis=0, keepdims=True)
    for m, w in ((cpl.T, wf), (cpl, wa)):
        scaled = -dinv * (jnp.where(eye, 0.0, m) - jnp.where(beside, CHAIN, 0.0))
        hi, lo = two(scaled)
        w[0:CELLS, 0:CELLS] = hi
        w[0:CELLS, CELLS:] = lo
        w[CELLS:, 0:CELLS] = hi
        w[CELLS:, CELLS:] = lo

    owner_row = own_ref[...]
    slot_row = slot_ref[...]
    owner_col = column(owner_row.astype(f32)).astype(i32)
    earlier = (owner_col == owner_row) & (iota((BLOCKS, BLOCKS), 0) < iota((BLOCKS, BLOCKS), 1))
    rank = jnp.sum(jnp.where(earlier, 1.0, 0.0), axis=0, keepdims=True).astype(i32)
    place = owner_row * CAP + rank
    pick = jnp.where(iota((nm * CAP, BLOCKS), 0) == place, 1.0, 0.0)
    qmat[...] = pick.astype(bf16)
    slot_of = jnp.sum(pick * (slot_row + 1).astype(f32), axis=1, keepdims=True)
    slots[...] = jnp.broadcast_to(slot_of, (nm * CAP, CELLS)).reshape(nm, CAP, CELLS)

    own_table.wait()
    for z in [0] + far_z[::-1]:
        owner = z_at[z] + mx
        if z:
            remote(
                table_rows(owner), table_rows(owner), ag_send.at[0], ag_recv.at[lax.div(z_at[z], NX)], c=other
            ).wait_recv()
        for x in far_x:
            remote(
                table_rows(owner), table_rows(owner), fan_send.at[0], fan_recv.at[0], m=z_at[0] + x_at[x]
            ).start()

    for z, x in far:
        m = z_at[z] + x_at[x]
        remote(slots.at[m], slots_in.at[me], sl_send.at[0], sl_recv.at[0], m=m).start()

    bytes_of(near, small_send.at[0], small_recv.at[0]).wait_recv()
    own3 = jnp.concatenate([near[0, 0], owner_row, near[1, 0]] + [owner_row] * 5, axis=0)
    slot3 = jnp.concatenate([near[0, 1], slot_row, near[1, 1]] + [slot_row] * 5, axis=0)
    index_v[...] = own3 * half_rows + (slot3 & (half_rows - 1))
    to_scalars = pltpu.make_async_copy(index_v, index_s, index_sem)
    to_scalars.start()

    mine = jnp.where((slot3 >> 5) == core, 1.0, 0.0)
    wide = (HALO, BLOCKS)
    col_l = jnp.sum(jnp.where(iota(wide, 0) + BLOCKS - HALO == iota(wide, 1), mine[0:1], 0.0), axis=1, keepdims=True)
    col_r = jnp.sum(jnp.where(iota(wide, 0) == iota(wide, 1), mine[2:3], 0.0), axis=1, keepdims=True)
    choose[0:HALO, :] = jnp.broadcast_to(col_l, (HALO, CELLS))
    choose[HALO:HALO + BLOCKS, :] = jnp.broadcast_to(column(mine[1:2]), (BLOCKS, CELLS))
    choose[HALO + BLOCKS:, :] = jnp.broadcast_to(col_r, (HALO, CELLS))

    obs_swap.wait_recv()
    bytes_of(obs_near, obs_send.at[0], obs_recv.at[0]).wait_recv()
    odd = iota((8, CELLS), 0) % 2

    def receivers(cells, base, obs_at):
        block = (cells >> 7) + base - HALF * odd
        lane = jnp.where(iota((CELLS, CELLS), 0) == (cells & (CELLS - 1)), 1.0, 0.0).astype(bf16)
        values = []
        for p in range(2):
            rows = [obs_at[p, pl.ds(4 * core + s, 1), :] for s in range(4)]
            values.append(jnp.concatenate([rows[r // 2] for r in range(8)], axis=0))
        return block, lane, values

    def scatter(block, lane, values, i):
        at = jnp.tile(block, (8, 1)) == 8 * i + (iota((64, CELLS), 0) >> 3)
        twice = jnp.concatenate([lane, lane], axis=1)
        res = []
        for v in values:
            hi, lo = two(jnp.where(at, jnp.tile(v, (8, 1)), 0.0))
            res.append(dot_t(jnp.concatenate([hi, lo], axis=1), twice))
        return res, dot_t(jnp.where(at, 1.0, 0.0).astype(bf16), lane)

    here = receivers(rcv_ref[...], HALO, obs_own)

    @pl.loop(0, HALF // 8)
    def _(i):
        res, cnt = scatter(*here, i)
        rows = pl.ds(pl.multiple_of(64 * i, 64), 64)
        heard[0, rows, :] = res[0]
        heard[1, rows, :] = res[1]
        count[rows, :] = cnt

    last = HALF // 8 - 1
    for side, base, i in ((0, HALO - BLOCKS, 0), (1, HALO + BLOCKS, last)):
        res, cnt = scatter(*receivers(near[side, 2], base, obs_near.at[side]), i)
        rows = slice(64 * i, 64 * i + 64)
        heard[0, rows, :] += res[0]
        heard[1, rows, :] += res[1]
        count[rows, :] += cnt

    for c in own_src:
        c.wait()
    bytes_of(stage.at[0:4 * BLOCKS, :], ex_send.at[0], ex_recv.at[0]).wait_recv()
    bytes_of(stage.at[0:16 * HALO, :], halo_send.at[0], halo_recv.at[0]).wait_recv()

    even_rows = iota((64, CELLS), 0) % 2 == 0
    keep_l = jnp.where(even_rows & (me == 0), 0.0, 1.0)
    keep_r = jnp.where(jnp.logical_not(even_rows) & (me == nm - 1), 0.0, 1.0)

    def kept(i, x):
        if isinstance(i, int):
            return x * keep_l if i == 0 else x * keep_r if i == last else x
        return x * jnp.where(i == 0, keep_l, jnp.where(i == last, keep_r, 1.0))

    def at64(i, first=0):
        return slice(first + 64 * i, first + 64 * i + 64) if isinstance(i, int) else pl.ds(
            pl.multiple_of(first + 64 * i, 8), 64)

    def put(b, p, i, x):
        b[p, at64(i, 8), :] = x
        hi, lo = two(x)
        lhs_hi[at64(2 * i + p), :] = hi
        lhs_lo[at64(2 * i + p), :] = lo

    def seams(b):
        top = iota((8, CELLS), 0) % 2 == 0
        for p in range(2):
            end = b[p, ROWS:ROWS + 8, :]
            start = b[p, 8:16, :]
            b[p, 0:8, :] = jnp.where(top, 0.0, pltpu.roll(end, 1, axis=0))
            b[p, ROWS + 8:ROWS + 16, :] = jnp.where(top, pltpu.roll(start, 7, axis=0), 0.0)

    @pl.loop(0, HALF // 8)
    def _(i):
        for p in range(2):
            x = jnp.concatenate(
                [stage[pl.ds(p * (4 * STAGE) + 8 * i + j, 8, stride=HALF), :] for j in range(8)], axis=0
            )
            x = kept(i, x * dinv)
            q[0, p, at64(i), :] = x
            put(fwd_a, p, i, x)

    seams(fwd_a)

    bytes_of(table.at[0:nz * (NX - 1) * half_rows, :], fan_send.at[0], fan_recv.at[0]).wait_recv()
    to_scalars.wait()

    def pick_rows(first, source, lane):
        picked[pl.ds(first, 8), :] = jnp.concatenate(
            [table[pl.ds(index_s[source, lane + j], 1), :] for j in range(8)], axis=0
        )

    pick_rows(0, 0, BLOCKS - HALO)
    pick_rows(HALO + BLOCKS, 2, 0)

    @pl.loop(0, BLOCKS // 8)
    def _(i):
        pick_rows(pl.multiple_of(HALO + 8 * i, 8), 1, 8 * i)

    swap = remote(picked, theirs, pick_send.at[0], pick_recv.at[0], c=other)
    swap.start()
    swap.wait_recv()
    wsig[...] = OMEGA * jnp.exp(jnp.where(choose[...] > 0.5, picked[...], theirs[...]))

    @pl.loop(0, HALF // 8)
    def _(i):
        rows = []
        for j in range(8):
            a = jnp.broadcast_to(wsig[pl.ds(8 * i + j, 1), :], (8, CELLS))
            b = jnp.broadcast_to(wsig[pl.ds(HALF + 8 * i + j, 1), :], (8, CELLS))
            rows.append(jnp.where(odd == 0, a, b))
        cross[at64(i), :] = kept(i, jnp.concatenate(rows, axis=0) * dinv)

    lane_row = iota((1, CELLS), 1)
    at_first = jnp.where(lane_row == 0, CHAIN * dinv, 0.0)
    at_last = jnp.where(lane_row == CELLS - 1, CHAIN * dinv, 0.0)

    def sweep(old, new, qk, sign, weights):
        for first in range(0, HALF // 8, GROUP):
            rows = slice(128 * first, 128 * (first + GROUP))
            prod = dot(jnp.concatenate([lhs_hi[rows, :], lhs_lo[rows, :]], axis=1), weights[...])
            prod = prod[:, 0:CELLS] + prod[:, CELLS:]
            for i in range(first, first + GROUP):
                turn = cross[at64(i), :]
                for p in range(2):
                    k = 2 * (i - first) + p
                    before = old[p, at64(i), :]
                    after = old[p, at64(i, 16), :]
                    both = turn * old[1 - p, at64(i, 8), :]
                    x = q[qk, p, at64(i), :] + prod[64 * k:64 * k + 64, :]
                    x = x + at_first * pltpu.roll(before, 1, axis=1) + at_last * pltpu.roll(after, CELLS - 1, axis=1)
                    x = x + both if (sign > 0) == (p == 0) else x - both
                    put(new, p, i, kept(i, x))
        seams(new)

    def sweeps(a, b, *args):
        sweep(a, b, *args)

        @pl.loop(0, ITERS // 2 - 1)
        def _(k):
            sweep(b, a, *args)
            sweep(a, b, *args)

    sweeps(fwd_a, fwd_b, 0, 1, wf)

    @pl.loop(0, HALF // 8)
    def _(i):
        for p in range(2):
            x = count[at64(i), :] * fwd_b[p, at64(i, 8), :] - heard[p, at64(i), :]
            x = kept(i, x * dinv)
            q[1, p, at64(i), :] = x
            put(adj_a, p, i, x)

    seams(adj_a)

    sweeps(adj_a, adj_b, 1, -1, wa)

    for i in range(HALF // 8):
        psum_buf[at64(i), :] = (
            adj_b[0, at64(i, 8), :] * fwd_b[1, at64(i, 8), :]
            - adj_b[1, at64(i, 8), :] * fwd_b[0, at64(i, 8), :]
        )

    for i in range(BLOCKS // 16):
        for h in range(2):
            first = 8 * (8 * i + (HALO if h == 0 else 0)) + h
            acc = psum_buf[pl.ds(first, 8, stride=8), :]
            for s in range(1, 4):
                acc = acc + psum_buf[pl.ds(first + 2 * s, 8, stride=8), :]
            at = 8 * i + (HALF - HALO) * h
            part[at:at + 8, :] = acc * wsig[HALO + at:HALO + at + 8, :]

    hi, mid, lo = three(part[...])
    sel = qmat[...]
    packed = dot(sel, hi) + dot(sel, mid) + dot(sel, lo)
    pack[...] = packed.reshape(nm, CAP, CELLS)

    for z, x in far:
        m = z_at[z] + x_at[x]
        remote(pack.at[m], pack_in.at[me], gp_send.at[0], gp_recv.at[0], m=m).start()

    pack_in[me] = pack[me]
    bytes_of(slots.at[0:nm - 1], sl_send.at[0], sl_recv.at[0]).wait_recv()
    slots_in[me] = slots[me]
    slot_in = slots_in[...].reshape(nm * CAP, CELLS)
    hit = jnp.where(slot_in == (iota((nm * CAP, CELLS), 1) + 1).astype(f32), 1.0, 0.0)
    hits[...] = hit.T.astype(bf16)

    bytes_of(table.at[0:(nz - 1) * half_rows, :], ag_send.at[0], ag_recv.at[0]).wait_send()
    bytes_of(near, small_send.at[0], small_recv.at[0]).wait_send()
    bytes_of(stage.at[0:4 * BLOCKS, :], ex_send.at[0], ex_recv.at[0]).wait_send()
    obs_swap.wait_send()
    bytes_of(stage.at[0:16 * HALO, :], halo_send.at[0], halo_recv.at[0]).wait_send()
    bytes_of(obs_near, obs_send.at[0], obs_recv.at[0]).wait_send()
    bytes_of(table.at[0:nz * (NX - 1) * half_rows, :], fan_send.at[0], fan_recv.at[0]).wait_send()
    swap.wait_send()
    bytes_of(slots.at[0:nm - 1], sl_send.at[0], sl_recv.at[0]).wait_send()

    bytes_of(pack.at[0:nm - 1], gp_send.at[0], gp_recv.at[0]).wait_recv()
    hi, mid, lo = three(pack_in[...].reshape(nm * CAP, CELLS))
    sel = hits[0:OWNED, :]
    grad[...] = dot(sel, hi) + dot(sel, mid) + dot(sel, lo)

    mine_half = pl.ds(pl.multiple_of(core * half_rows, 8), half_rows)
    their_half = pl.ds(pl.multiple_of(other * half_rows, 8), half_rows)
    cores = remote(grad.at[their_half, :], grad_in, gr_send.at[0], gr_recv.at[0], c=other)
    cores.start()
    cores.wait_recv()
    line[grp] = grad[mine_half, :] + grad_in[...]
    for d in far_g:
        remote(line.at[grp], line.at[grp], ln_send.at[0], ln_recv.at[0], g=g_at[d]).start()
    cores.wait_send()
    bytes_of(pack.at[0:nm - 1], gp_send.at[0], gp_recv.at[0]).wait_send()
    bytes_of(line.at[0:ng - 1], ln_send.at[0], ln_recv.at[0]).wait_recv()

    summed = line[0]
    for g in range(1, ng):
        summed = summed + line[g]
    total[...] = summed
    back = remote(total, total_in, to_send.at[0], to_recv.at[0], c=other)
    back.start()
    out_ref[mine_half, :] = summed
    bytes_of(line.at[0:ng - 1], ln_send.at[0], ln_recv.at[0]).wait_send()
    back.wait()
    out_ref[their_half, :] = total_in[...]


def local(log_sigma, block_owner, block_slot, coupling, sources, rcv_cell, observed):
    nm, ng = lax.axis_size("mesh"), lax.axis_size("group")
    vmem, hbm, dma = pltpu.VMEM, pl.BlockSpec(memory_space=pl.ANY), pltpu.SemaphoreType.DMA
    inside = pl.BlockSpec(memory_space=pltpu.VMEM)
    nz = nm // NX
    return pl.pallas_call(
        functools.partial(kernel, ng, nm),
        out_shape=jax.ShapeDtypeStruct((OWNED, CELLS), f32),
        in_specs=[inside] * 5 + [hbm] * 2,
        out_specs=inside,
        scratch_shapes=[
            vmem((8 * STAGE, CELLS), f32),
            vmem((nm * OWNED // 2, CELLS), f32),
            vmem((2, 3, 1, BLOCKS), i32),
            vmem((2, S, CELLS), f32),
            vmem((2, 2, S, CELLS), f32),
            vmem((8, BLOCKS), i32),
            pltpu.SMEM((8, BLOCKS), i32),
            vmem((STAGE, CELLS), f32),
            vmem((STAGE, CELLS), f32),
            vmem((STAGE, CELLS), f32),
            vmem((2, ROWS + 16, CELLS), f32),
            vmem((2, ROWS + 16, CELLS), f32),
            vmem((2, ROWS + 16, CELLS), f32),
            vmem((2, ROWS + 16, CELLS), f32),
            vmem((2 * ROWS, CELLS), bf16),
            vmem((2 * ROWS, CELLS), bf16),
            vmem((2, 2, ROWS, CELLS), f32),
            vmem((ROWS, CELLS), f32),
            vmem((STAGE, CELLS), f32),
            vmem((CELLS, nm * CAP), bf16),
            vmem((2, ROWS, CELLS), f32),
            vmem((ROWS, CELLS), f32),
            vmem((2 * CELLS, 2 * CELLS), bf16),
            vmem((2 * CELLS, 2 * CELLS), bf16),
            vmem((nm * CAP, BLOCKS), bf16),
            vmem((ROWS, CELLS), f32),
            vmem((BLOCKS, CELLS), f32),
            vmem((nm, CAP, CELLS), f32),
            vmem((nm, CAP, CELLS), f32),
            vmem((nm, CAP, CELLS), f32),
            vmem((nm, CAP, CELLS), f32),
            vmem((OWNED, CELLS), f32),
            vmem((OWNED // 2, CELLS), f32),
            vmem((ng, OWNED // 2, CELLS), f32),
            vmem((OWNED // 2, CELLS), f32),
            vmem((OWNED // 2, CELLS), f32),
            dma((6,)),
            dma((2,)), dma((2,)),
            dma((1,)), dma((1,)),
            dma((1,)), dma((1,)),
            dma((1,)), dma((1,)),
            dma((1,)), dma((nz,)),
            dma((1,)), dma((1,)),
            dma((1,)), dma((1,)),
            dma((1,)), dma((1,)),
            dma((1,)), dma((1,)),
            dma((1,)), dma((1,)),
            dma((1,)), dma((1,)),
            dma((1,)), dma((1,)),
            dma(()),
        ],
        compiler_params=pltpu.CompilerParams(collective_id=0, has_side_effects=True),
    )(
        block_owner.reshape(1, BLOCKS), block_slot, rcv_cell, observed.reshape(S, CELLS), coupling, log_sigma, sources.reshape(S, BLOCKS, CELLS)
    )


def solution(mesh):
    in_specs = (
        P("mesh", None),
        P("group", "mesh", None),
        P("group", "mesh"),
        P(),
        P("group", "comp", None, "mesh", None),
        P("group", "mesh"),
        P("group", "comp", None, "mesh"),
    )
    return jax.shard_map(local, mesh=mesh, in_specs=in_specs, out_specs=P("mesh", None), check_vma=False)
```

time: 534 us -> 53.2 us (0.10)
  waiting for transfers between devices: 311 us -> 0 us
  starting transfers between devices: 118 us -> 0 us
  Pallas kernels: 0 us -> 51.6 us
  blocking collectives: 48.6 us -> 0 us
  between operations: 14 us -> 0.01 us
  other arithmetic: 13.8 us -> 0 us
  local copies, waits for them, and re-layouts: 14.9 us -> 1.38 us
  matrix products: 10.1 us -> 0 us
    reduce_scatter x1 -> x0, waiting for transfers between devices: 237 us -> none  [local(): lax.psum_scatter(jnp.zeros((inv_rows * lax.axis_size('mesh'), CELLS), jnp...]
    ppermute x34 -> x0, starting transfers between devices: 118 us -> none  [the longest x11 60.6 us: with_halo(): before = lax.ppermute(last, axis, up)]
    all_gather x1 -> x0, waiting for transfers between devices: 68.6 us -> none  [local(): gathered = lax.all_gather(log_sigma, 'mesh', axis=0, tiled=True)]
    pallas_call x0 -> x1, Pallas kernels: none -> 51.6 us  [local(): pl.pallas_call(functools.partial(kernel, ng, nm), out_shape=jax.ShapeDtyp...]
    psum x1 -> x0, blocking collectives: 48.6 us -> none  [local(): return lax.psum(owned, ('group', 'comp'))]
    dot_general x12 -> x0, matrix products: 10.1 us -> none  [cell_product(): jnp.einsum('...bj,ij->...bi', shaped, matrix, precision=lax.Precision.HIG...]
    scatter-add x2 -> x0, other arithmetic: 8.05 us -> none  [the longest x1 5.95 us: local(): adjoint_src = jnp.zeros_like(right).at[:, receivers].add(misfit)]
    scatter-add x1 -> x0, local copies, waits for them, and re-layouts: 5.54 us -> none  [local(): adjoint_src = jnp.zeros_like(right).at[:, receivers].add(misfit)]
  transfers between devices with their start and end apart: 36 -> 0, of which waited for: 12 -> 0; matrix products, arithmetic and copies ran while one was open for 2% -> 0% of each run, Pallas kernels for 0% -> 0%
where the time goes in v2:
time: 53.2 us; the launch traced here: 53 us
  Pallas kernels  51.6 us (97%)
  local copies, waits for them, and re-layouts  1.38 us (3%)
    pallas_call x1, Pallas kernels, local(): pl.pallas_call(functools.partial(kernel, ng, nm), out_shape=jax.ShapeDtyp...  51.6 us
    unnamed x1, local copies, waits for them, and re-layouts  1.38 us

profile of v2, /device:TPU:1, one launch (start us, length us, event | category | flops | bytes accessed | tf_op | source)
XLA Modules:
  0.0 53.0 jit_solution(14187126493912386522)
XLA Ops:
  0.0 51.6 %shard_map.73 = f32[64,128]{1,0:T(8,128)} custom-call(s32[1,128]{1,0:T(1,128)} %bitcast.5, s32[1,128]{1,0:T(1,128)} %slot_ref.1, s32[1,128]{1,0:T(1,128)} %rcv_ref.1, f32[8,128]{1,0:T(8,128)} %bitcast.4, f32[128,128]{1,0:T(8,128)} %cpl_ref.1, f32[64,128]{1,0:T(8,128)} %ls_ref.1, f32[8,128,128]{2,1,0:T(8,128)} %bitcast.3), custom_call_target="tpu_custom_call" | custom-call | tf_op jit(solution)/shard_map/pallas_call | solution.py:438
  51.6 1.4 %copy.9 = f32[64,128]{1,0:T(8,128)} copy(f32[64,128]{1,0:T(8,128)} %shard_map.73) | data formatting | bytes 65536

commit v3 on v2

--- a/solution.py
+++ b/solution.py
@@ -56,8 +56,8 @@
 
 
 def kernel(
-    ng, nm, own_ref, slot_ref, rcv_ref, obs_ref, cpl_ref, ls_ref, src_ref, out_ref,
-    stage, table, near, obs_own, obs_near, index_v, index_s, picked, theirs, choose,
+    ng, nm, own_ref, slot_ref, rcv_ref, obs_ref, cpl_ref, ls_ref, src_ref, low_ref, high_ref,
+    stage, table, near, self_v, cpl_v, obs_own, obs_near, index_v, index_s, picked, theirs, choose,
     fwd_a, fwd_b, adj_a, adj_b, lhs_hi, lhs_lo, q, cross, wsig, hits, heard, count, wf, wa, qmat, psum_buf, part,
     slots, slots_in, pack, pack_in, grad, grad_in, line, total, total_in,
     local_sem, ex_send, ex_recv, halo_send, halo_recv, obs_send, obs_recv, small_send, small_recv,
@@ -99,12 +99,15 @@
         where = (grp if g is None else g, me if m is None else m, core if c is None else c)
         pl.semaphore_signal(barrier, inc=1, device_id=where, device_id_type=pl.DeviceIdType.MESH)
 
-    for z, x in far:
-        greet(m=z_at[z] + x_at[x])
+    for z in far_z:
+        greet(m=z_at[z] + mx)
     for d in far_g:
         greet(g=g_at[d])
-    greet(m=left, c=other)
-    greet(m=right, c=other)
+    for x in far_x:
+        greet(m=z_at[0] + x_at[x])
+    for m in (left, right):
+        for c in (core, other):
+            greet(m=m, c=c)
     greet(c=other)
 
     half_rows = OWNED // 2
@@ -122,10 +125,16 @@
         pltpu.make_async_copy(src_ref.at[4 * core + s], stage_rows(core, s, HALO, BLOCKS), local_sem.at[s + 2])
         for s in range(4)
     ]
-    for c in own_src:
+    own_cells = [
+        pltpu.make_async_copy(ref, self_v.at[k], local_sem.at[6 + k])
+        for k, ref in enumerate((own_ref, slot_ref, rcv_ref))
+    ]
+    own_cpl = pltpu.make_async_copy(cpl_ref, cpl_v, local_sem.at[9])
+    own_obs = pltpu.make_async_copy(obs_ref, obs_own.at[core], local_sem.at[0])
+    for c in [own_cpl, own_obs] + own_cells + own_src:
         c.start()
 
-    pl.semaphore_wait(barrier, nm - 1 + ng - 1 + 3)
+    pl.semaphore_wait(barrier, nz - 1 + NX - 1 + ng - 1 + 5)
 
     for z in far_z:
         remote(ls_ref.at[own_half, :], table_rows(me), ag_send.at[0], ag_recv.at[mz], m=z_at[z] + mx).start()
@@ -147,11 +156,11 @@
                     halo_send.at[0], halo_recv.at[0], m=m, c=c,
                 ).start()
             remote(obs_ref, obs_near.at[side, core], obs_send.at[0], obs_recv.at[0], m=m, c=c).start()
-    obs_own[core] = obs_ref[...]
 
     eye = iota((CELLS, CELLS), 0) == iota((CELLS, CELLS), 1)
     beside = jnp.abs(iota((CELLS, CELLS), 0) - iota((CELLS, CELLS), 1)) == 1
-    cpl = cpl_ref[...]
+    own_cpl.wait()
+    cpl = cpl_v[...]
     dinv = 1.0 / jnp.sum(jnp.where(eye, cpl, 0.0), axis=0, keepdims=True)
     for m, w in ((cpl.T, wf), (cpl, wa)):
         scaled = -dinv * (jnp.where(eye, 0.0, m) - jnp.where(beside, CHAIN, 0.0))
@@ -161,8 +170,10 @@
         w[CELLS:, 0:CELLS] = hi
         w[CELLS:, CELLS:] = lo
 
-    owner_row = own_ref[...]
-    slot_row = slot_ref[...]
+    for c in own_cells:
+        c.wait()
+    owner_row = self_v[0]
+    slot_row = self_v[1]
     owner_col = column(owner_row.astype(f32)).astype(i32)
     earlier = (owner_col == owner_row) & (iota((BLOCKS, BLOCKS), 0) < iota((BLOCKS, BLOCKS), 1))
     rank = jnp.sum(jnp.where(earlier, 1.0, 0.0), axis=0, keepdims=True).astype(i32)
@@ -184,10 +195,6 @@
                 table_rows(owner), table_rows(owner), fan_send.at[0], fan_recv.at[0], m=z_at[0] + x_at[x]
             ).start()
 
-    for z, x in far:
-        m = z_at[z] + x_at[x]
-        remote(slots.at[m], slots_in.at[me], sl_send.at[0], sl_recv.at[0], m=m).start()
-
     bytes_of(near, small_send.at[0], small_recv.at[0]).wait_recv()
     own3 = jnp.concatenate([near[0, 0], owner_row, near[1, 0]] + [owner_row] * 5, axis=0)
     slot3 = jnp.concatenate([near[0, 1], slot_row, near[1, 1]] + [slot_row] * 5, axis=0)
@@ -203,6 +210,7 @@
     choose[HALO:HALO + BLOCKS, :] = jnp.broadcast_to(column(mine[1:2]), (BLOCKS, CELLS))
     choose[HALO + BLOCKS:, :] = jnp.broadcast_to(col_r, (HALO, CELLS))
 
+    own_obs.wait()
     obs_swap.wait_recv()
     bytes_of(obs_near, obs_send.at[0], obs_recv.at[0]).wait_recv()
     odd = iota((8, CELLS), 0) % 2
@@ -225,7 +233,7 @@
             res.append(dot_t(jnp.concatenate([hi, lo], axis=1), twice))
         return res, dot_t(jnp.where(at, 1.0, 0.0).astype(bf16), lane)
 
-    here = receivers(rcv_ref[...], HALO, obs_own)
+    here = receivers(self_v[2], HALO, obs_own)
 
     @pl.loop(0, HALF // 8)
     def _(i):
@@ -304,6 +312,11 @@
 
     swap = remote(picked, theirs, pick_send.at[0], pick_recv.at[0], c=other)
     swap.start()
+
+    for z, x in far:
+        m = z_at[z] + x_at[x]
+        remote(slots.at[m], slots_in.at[me], sl_send.at[0], sl_recv.at[0], m=m).start()
+
     swap.wait_recv()
     wsig[...] = OMEGA * jnp.exp(jnp.where(choose[...] > 0.5, picked[...], theirs[...]))
 
@@ -418,16 +431,19 @@
     bytes_of(pack.at[0:nm - 1], gp_send.at[0], gp_recv.at[0]).wait_send()
     bytes_of(line.at[0:ng - 1], ln_send.at[0], ln_recv.at[0]).wait_recv()
 
-    summed = line[0]
-    for g in range(1, ng):
-        summed = summed + line[g]
-    total[...] = summed
+    for k in range(2):
+        summed = line[k * (ng // 2)]
+        for g in range(k * (ng // 2) + 1, (k + 1) * (ng // 2)):
+            summed = summed + line[g]
+        total[k] = summed
     back = remote(total, total_in, to_send.at[0], to_recv.at[0], c=other)
     back.start()
-    out_ref[mine_half, :] = summed
+    low_ref[mine_half, :] = total[0]
+    high_ref[mine_half, :] = total[1]
     bytes_of(line.at[0:ng - 1], ln_send.at[0], ln_recv.at[0]).wait_send()
     back.wait()
-    out_ref[their_half, :] = total_in[...]
+    low_ref[their_half, :] = total_in[0]
+    high_ref[their_half, :] = total_in[1]
 
 
 def local(log_sigma, block_owner, block_slot, coupling, sources, rcv_cell, observed):
@@ -435,15 +451,17 @@
     vmem, hbm, dma = pltpu.VMEM, pl.BlockSpec(memory_space=pl.ANY), pltpu.SemaphoreType.DMA
     inside = pl.BlockSpec(memory_space=pltpu.VMEM)
     nz = nm // NX
-    return pl.pallas_call(
+    low, high = pl.pallas_call(
         functools.partial(kernel, ng, nm),
-        out_shape=jax.ShapeDtypeStruct((OWNED, CELLS), f32),
-        in_specs=[inside] * 5 + [hbm] * 2,
-        out_specs=inside,
+        out_shape=[jax.ShapeDtypeStruct((OWNED, CELLS), f32)] * 2,
+        in_specs=[hbm] * 7,
+        out_specs=[inside] * 2,
         scratch_shapes=[
             vmem((8 * STAGE, CELLS), f32),
             vmem((nm * OWNED // 2, CELLS), f32),
             vmem((2, 3, 1, BLOCKS), i32),
+            vmem((3, 1, BLOCKS), i32),
+            vmem((CELLS, CELLS), f32),
             vmem((2, S, CELLS), f32),
             vmem((2, 2, S, CELLS), f32),
             vmem((8, BLOCKS), i32),
@@ -475,9 +493,9 @@
             vmem((OWNED, CELLS), f32),
             vmem((OWNED // 2, CELLS), f32),
             vmem((ng, OWNED // 2, CELLS), f32),
-            vmem((OWNED // 2, CELLS), f32),
-            vmem((OWNED // 2, CELLS), f32),
-            dma((6,)),
+            vmem((2, OWNED // 2, CELLS), f32),
+            vmem((2, OWNED // 2, CELLS), f32),
+            dma((10,)),
             dma((2,)), dma((2,)),
             dma((1,)), dma((1,)),
             dma((1,)), dma((1,)),
@@ -496,6 +514,7 @@
     )(
         block_owner.reshape(1, BLOCKS), block_slot, rcv_cell, observed.reshape(S, CELLS), coupling, log_sigma, sources.reshape(S, BLOCKS, CELLS)
     )
+    return low + high
 
 
 def solution(mesh):

time: 53.2 us -> 50.1 us (0.942)
  Pallas kernels: 51.6 us -> 48.5 us
  other arithmetic: 0 us -> 1.4 us
  local copies, waits for them, and re-layouts: 1.38 us -> 0 us
    pallas_call x1, Pallas kernels: 51.6 us -> 48.5 us  [local(): pl.pallas_call(functools.partial(kernel, ng, nm), out_shape=[jax.ShapeDty...]
    add x0 -> x1, other arithmetic: none -> 1.4 us  [local(): return low + high]
    unnamed x1 -> x0, local copies, waits for them, and re-layouts: 1.38 us -> none
where the time goes in v3:
time: 50.1 us; the launch traced here: 49.9 us
  Pallas kernels  48.5 us (97%)
  other arithmetic  1.4 us (3%)
    pallas_call x1, Pallas kernels, local(): pl.pallas_call(functools.partial(kernel, ng, nm), out_shape=[jax.ShapeDty...  48.5 us
    add x1, other arithmetic, local(): return low + high  1.4 us

profile of v3, /device:TPU:1, one launch (start us, length us, event | category | flops | bytes accessed | tf_op | source)
XLA Modules:
  0.0 49.9 jit_solution(16145727146129756965)
XLA Ops:
  0.0 48.5 %shard_map.73 = (f32[64,128]{1,0:T(8,128)}, f32[64,128]{1,0:T(8,128)}) custom-call(s32[1,128]{1,0:T(1,128)} %bitcast.5, s32[1,128]{1,0:T(1,128)} %slot_ref.1, s32[1,128]{1,0:T(1,128)} %rcv_ref.1, f32[8,128]{1,0:T(8,128)} %bitcast.4, f32[128,128]{1,0:T(8,128)} %cpl_ref.1, f32[64,128]{1,0:T(8,128)} %ls_ref.1, f32[8,128,128]{2,1,0:T(8,128)} %bitcast.3), custom_call_target="tpu_custom_call" | custom-call | tf_op jit(solution)/shard_map/pallas_call | solution.py:454
  48.5 1.4 %add.3 = f32[64,128]{1,0:T(8,128)} add(f32[64,128]{1,0:T(8,128)} %get-tuple-element.7, f32[64,128]{1,0:T(8,128)} %get-tuple-element.8) | non-fusion elementwise | flops 8192 | bytes 98304 | tf_op jit(solution)/shard_map/add | solution.py:517

commit v4 on v3

--- a/solution.py
+++ b/solution.py
@@ -50,19 +50,30 @@
     return lax.dot_general(a, b, NT, preferred_element_type=f32)
 
 
+def cell_of(lane):
+    return jnp.where(lane == CELLS // 2, CELLS - 1, jnp.where(lane == CELLS - 1, CELLS // 2, lane))
+
+
+def reorder(x):
+    lane = iota(x.shape, 1)
+    up = pltpu.roll(x, CELLS // 2 + 1, axis=1)
+    down = pltpu.roll(x, CELLS // 2 - 1, axis=1)
+    return jnp.where(lane == CELLS // 2, up, jnp.where(lane == CELLS - 1, down, x))
+
+
 def column(row):
     n = row.shape[1]
     return jnp.sum(jnp.where(iota((n, n), 0) == iota((n, n), 1), row, 0.0), axis=1, keepdims=True)
 
 
 def kernel(
-    ng, nm, own_ref, slot_ref, rcv_ref, obs_ref, cpl_ref, ls_ref, src_ref, low_ref, high_ref,
+    ng, nm, own_ref, slot_ref, rcv_ref, obs_ref, cpl_ref, ls_ref, src_ref, out_ref,
     stage, table, near, self_v, cpl_v, obs_own, obs_near, index_v, index_s, picked, theirs, choose,
     fwd_a, fwd_b, adj_a, adj_b, lhs_hi, lhs_lo, q, cross, wsig, hits, heard, count, wf, wa, qmat, psum_buf, part,
-    slots, slots_in, pack, pack_in, grad, grad_in, line, total, total_in,
+    slots, slots_in, pack, pack_in, line, total, total_in,
     local_sem, ex_send, ex_recv, halo_send, halo_recv, obs_send, obs_recv, small_send, small_recv,
     ag_send, ag_recv, fan_send, fan_recv, pick_send, pick_recv, sl_send, sl_recv, gp_send, gp_recv,
-    gr_send, gr_recv, ln_send, ln_recv, to_send, to_recv, index_sem,
+    ln_send, ln_recv, to_send, to_recv, index_sem,
 ):
     me = lax.axis_index("mesh")
     core = lax.axis_index("comp")
@@ -136,7 +147,7 @@
 
     pl.semaphore_wait(barrier, nz - 1 + NX - 1 + ng - 1 + 5)
 
-    for z in far_z:
+    for z in far_z[::-1]:
         remote(ls_ref.at[own_half, :], table_rows(me), ag_send.at[0], ag_recv.at[mz], m=z_at[z] + mx).start()
 
     for side, m in ((0, right), (1, left)):
@@ -158,8 +169,13 @@
             remote(obs_ref, obs_near.at[side, core], obs_send.at[0], obs_recv.at[0], m=m, c=c).start()
 
     eye = iota((CELLS, CELLS), 0) == iota((CELLS, CELLS), 1)
-    beside = jnp.abs(iota((CELLS, CELLS), 0) - iota((CELLS, CELLS), 1)) == 1
+    square = (CELLS, CELLS)
+    beside = jnp.abs(cell_of(iota(square, 0)) - cell_of(iota(square, 1))) == 1
     own_cpl.wait()
+    cpl_v[...] = reorder(cpl_v[...])
+    mid_row, last_row = cpl_v[CELLS // 2:CELLS // 2 + 1, :], cpl_v[CELLS - 1:, :]
+    cpl_v[CELLS // 2:CELLS // 2 + 1, :] = last_row
+    cpl_v[CELLS - 1:, :] = mid_row
     cpl = cpl_v[...]
     dinv = 1.0 / jnp.sum(jnp.where(eye, cpl, 0.0), axis=0, keepdims=True)
     for m, w in ((cpl.T, wf), (cpl, wa)):
@@ -217,7 +233,7 @@
 
     def receivers(cells, base, obs_at):
         block = (cells >> 7) + base - HALF * odd
-        lane = jnp.where(iota((CELLS, CELLS), 0) == (cells & (CELLS - 1)), 1.0, 0.0).astype(bf16)
+        lane = jnp.where(cell_of(iota(square, 0)) == (cells & (CELLS - 1)), 1.0, 0.0).astype(bf16)
         values = []
         for p in range(2):
             rows = [obs_at[p, pl.ds(4 * core + s, 1), :] for s in range(4)]
@@ -289,7 +305,7 @@
             x = jnp.concatenate(
                 [stage[pl.ds(p * (4 * STAGE) + 8 * i + j, 8, stride=HALF), :] for j in range(8)], axis=0
             )
-            x = kept(i, x * dinv)
+            x = kept(i, reorder(x) * dinv)
             q[0, p, at64(i), :] = x
             put(fwd_a, p, i, x)
 
@@ -306,9 +322,8 @@
     pick_rows(0, 0, BLOCKS - HALO)
     pick_rows(HALO + BLOCKS, 2, 0)
 
-    @pl.loop(0, BLOCKS // 8)
-    def _(i):
-        pick_rows(pl.multiple_of(HALO + 8 * i, 8), 1, 8 * i)
+    for i in range(BLOCKS // 8):
+        pick_rows(HALO + 8 * i, 1, 8 * i)
 
     swap = remote(picked, theirs, pick_send.at[0], pick_recv.at[0], c=other)
     swap.start()
@@ -318,10 +333,9 @@
         remote(slots.at[m], slots_in.at[me], sl_send.at[0], sl_recv.at[0], m=m).start()
 
     swap.wait_recv()
-    wsig[...] = OMEGA * jnp.exp(jnp.where(choose[...] > 0.5, picked[...], theirs[...]))
-
-    @pl.loop(0, HALF // 8)
-    def _(i):
+    wsig[...] = OMEGA * jnp.exp(reorder(jnp.where(choose[...] > 0.5, picked[...], theirs[...])))
+
+    for i in range(HALF // 8):
         rows = []
         for j in range(8):
             a = jnp.broadcast_to(wsig[pl.ds(8 * i + j, 1), :], (8, CELLS))
@@ -330,8 +344,8 @@
         cross[at64(i), :] = kept(i, jnp.concatenate(rows, axis=0) * dinv)
 
     lane_row = iota((1, CELLS), 1)
-    at_first = jnp.where(lane_row == 0, CHAIN * dinv, 0.0)
-    at_last = jnp.where(lane_row == CELLS - 1, CHAIN * dinv, 0.0)
+    ends = jnp.where((lane_row == 0) | (lane_row == CELLS // 2), CHAIN * dinv, 0.0)
+    low_lane = iota((64, CELLS), 1) < CELLS // 4
 
     def sweep(old, new, qk, sign, weights):
         for first in range(0, HALF // 8, GROUP):
@@ -340,13 +354,12 @@
             prod = prod[:, 0:CELLS] + prod[:, CELLS:]
             for i in range(first, first + GROUP):
                 turn = cross[at64(i), :]
+                near_x = [old[p, 64 * i:64 * i + 80, :] for p in range(2)]
                 for p in range(2):
                     k = 2 * (i - first) + p
-                    before = old[p, at64(i), :]
-                    after = old[p, at64(i, 16), :]
-                    both = turn * old[1 - p, at64(i, 8), :]
-                    x = q[qk, p, at64(i), :] + prod[64 * k:64 * k + 64, :]
-                    x = x + at_first * pltpu.roll(before, 1, axis=1) + at_last * pltpu.roll(after, CELLS - 1, axis=1)
+                    end = jnp.where(low_lane, near_x[p][16:80], near_x[p][0:64])
+                    both = turn * near_x[1 - p][8:72]
+                    x = q[qk, p, at64(i), :] + prod[64 * k:64 * k + 64, :] + ends * pltpu.roll(end, CELLS // 2, axis=1)
                     x = x + both if (sign > 0) == (p == 0) else x - both
                     put(new, p, i, kept(i, x))
         seams(new)
@@ -361,8 +374,7 @@
 
     sweeps(fwd_a, fwd_b, 0, 1, wf)
 
-    @pl.loop(0, HALF // 8)
-    def _(i):
+    for i in range(HALF // 8):
         for p in range(2):
             x = count[at64(i), :] * fwd_b[p, at64(i, 8), :] - heard[p, at64(i), :]
             x = kept(i, x * dinv)
@@ -388,21 +400,29 @@
             at = 8 * i + (HALF - HALO) * h
             part[at:at + 8, :] = acc * wsig[HALO + at:HALO + at + 8, :]
 
-    hi, mid, lo = three(part[...])
+    hi, mid, lo = three(reorder(part[...]))
     sel = qmat[...]
     packed = dot(sel, hi) + dot(sel, mid) + dot(sel, lo)
     pack[...] = packed.reshape(nm, CAP, CELLS)
 
+    takes = lax.rem(mx, 2) == core
     for z, x in far:
         m = z_at[z] + x_at[x]
-        remote(pack.at[m], pack_in.at[me], gp_send.at[0], gp_recv.at[0], m=m).start()
-
-    pack_in[me] = pack[me]
+        remote(
+            pack.at[m], pack_in.at[core * nm + me], gp_send.at[0], gp_recv.at[0], m=m, c=lax.rem(x_at[x], 2)
+        ).start()
+    beside_me = remote(pack.at[me], pack_in.at[core * nm + me], gp_send.at[1], gp_recv.at[0], c=other)
+
+    @pl.when(jnp.logical_not(takes))
+    def _():
+        beside_me.start()
+
+    @pl.when(takes)
+    def _():
+        pack_in[core * nm + me] = pack[me]
+
     bytes_of(slots.at[0:nm - 1], sl_send.at[0], sl_recv.at[0]).wait_recv()
     slots_in[me] = slots[me]
-    slot_in = slots_in[...].reshape(nm * CAP, CELLS)
-    hit = jnp.where(slot_in == (iota((nm * CAP, CELLS), 1) + 1).astype(f32), 1.0, 0.0)
-    hits[...] = hit.T.astype(bf16)
 
     bytes_of(table.at[0:(nz - 1) * half_rows, :], ag_send.at[0], ag_recv.at[0]).wait_send()
     bytes_of(near, small_send.at[0], small_recv.at[0]).wait_send()
@@ -414,36 +434,39 @@
     swap.wait_send()
     bytes_of(slots.at[0:nm - 1], sl_send.at[0], sl_recv.at[0]).wait_send()
 
-    bytes_of(pack.at[0:nm - 1], gp_send.at[0], gp_recv.at[0]).wait_recv()
-    hi, mid, lo = three(pack_in[...].reshape(nm * CAP, CELLS))
-    sel = hits[0:OWNED, :]
-    grad[...] = dot(sel, hi) + dot(sel, mid) + dot(sel, lo)
-
-    mine_half = pl.ds(pl.multiple_of(core * half_rows, 8), half_rows)
-    their_half = pl.ds(pl.multiple_of(other * half_rows, 8), half_rows)
-    cores = remote(grad.at[their_half, :], grad_in, gr_send.at[0], gr_recv.at[0], c=other)
-    cores.start()
-    cores.wait_recv()
-    line[grp] = grad[mine_half, :] + grad_in[...]
-    for d in far_g:
-        remote(line.at[grp], line.at[grp], ln_send.at[0], ln_recv.at[0], g=g_at[d]).start()
-    cores.wait_send()
+    back = remote(total, total_in, to_send.at[0], to_recv.at[0], c=other)
+
+    @pl.when(takes)
+    def _():
+        slot_in = slots_in[...].reshape(nm * CAP, CELLS)
+        hit = jnp.where(slot_in == (iota((nm * CAP, CELLS), 1) + 1).astype(f32), 1.0, 0.0)
+        hits[...] = hit.T.astype(bf16)
+
+        bytes_of(pack_in.at[0:2 * nm - 1], gp_send.at[0], gp_recv.at[0]).wait_recv()
+        rows = (pack_in[0:nm] + pack_in[nm:2 * nm]).reshape(nm * CAP, CELLS)
+        hi, mid, lo = three(rows)
+        sel = hits[0:OWNED, :]
+        line[grp] = dot(sel, hi) + dot(sel, mid) + dot(sel, lo)
+
+        for d in far_g:
+            remote(line.at[grp], line.at[grp], ln_send.at[0], ln_recv.at[0], g=g_at[d]).start()
+        bytes_of(line.at[0:ng - 1], ln_send.at[0], ln_recv.at[0]).wait_recv()
+        summed = line[0]
+        for g in range(1, ng):
+            summed = summed + line[g]
+        total[...] = summed
+        back.start()
+        out_ref[...] = summed
+        bytes_of(line.at[0:ng - 1], ln_send.at[0], ln_recv.at[0]).wait_send()
+        back.wait_send()
+
+    @pl.when(jnp.logical_not(takes))
+    def _():
+        beside_me.wait_send()
+        back.wait_recv()
+        out_ref[...] = total_in[...]
+
     bytes_of(pack.at[0:nm - 1], gp_send.at[0], gp_recv.at[0]).wait_send()
-    bytes_of(line.at[0:ng - 1], ln_send.at[0], ln_recv.at[0]).wait_recv()
-
-    for k in range(2):
-        summed = line[k * (ng // 2)]
-        for g in range(k * (ng // 2) + 1, (k + 1) * (ng // 2)):
-            summed = summed + line[g]
-        total[k] = summed
-    back = remote(total, total_in, to_send.at[0], to_recv.at[0], c=other)
-    back.start()
-    low_ref[mine_half, :] = total[0]
-    high_ref[mine_half, :] = total[1]
-    bytes_of(line.at[0:ng - 1], ln_send.at[0], ln_recv.at[0]).wait_send()
-    back.wait()
-    low_ref[their_half, :] = total_in[0]
-    high_ref[their_half, :] = total_in[1]
 
 
 def local(log_sigma, block_owner, block_slot, coupling, sources, rcv_cell, observed):
@@ -451,11 +474,11 @@
     vmem, hbm, dma = pltpu.VMEM, pl.BlockSpec(memory_space=pl.ANY), pltpu.SemaphoreType.DMA
     inside = pl.BlockSpec(memory_space=pltpu.VMEM)
     nz = nm // NX
-    low, high = pl.pallas_call(
+    return pl.pallas_call(
         functools.partial(kernel, ng, nm),
-        out_shape=[jax.ShapeDtypeStruct((OWNED, CELLS), f32)] * 2,
+        out_shape=pltpu.VMEM((OWNED, CELLS), f32),
         in_specs=[hbm] * 7,
-        out_specs=[inside] * 2,
+        out_specs=inside,
         scratch_shapes=[
             vmem((8 * STAGE, CELLS), f32),
             vmem((nm * OWNED // 2, CELLS), f32),
@@ -489,12 +512,10 @@
             vmem((nm, CAP, CELLS), f32),
             vmem((nm, CAP, CELLS), f32),
             vmem((nm, CAP, CELLS), f32),
-            vmem((nm, CAP, CELLS), f32),
+            vmem((2 * nm, CAP, CELLS), f32),
+            vmem((ng, OWNED, CELLS), f32),
             vmem((OWNED, CELLS), f32),
-            vmem((OWNED // 2, CELLS), f32),
-            vmem((ng, OWNED // 2, CELLS), f32),
-            vmem((2, OWNED // 2, CELLS), f32),
-            vmem((2, OWNED // 2, CELLS), f32),
+            vmem((OWNED, CELLS), f32),
             dma((10,)),
             dma((2,)), dma((2,)),
             dma((1,)), dma((1,)),
@@ -504,8 +525,7 @@
             dma((1,)), dma((1,)),
             dma((1,)), dma((1,)),
             dma((1,)), dma((1,)),
-            dma((1,)), dma((1,)),
-            dma((1,)), dma((1,)),
+            dma((2,)), dma((1,)),
             dma((1,)), dma((1,)),
             dma((1,)), dma((1,)),
             dma(()),
@@ -514,7 +534,6 @@
     )(
         block_owner.reshape(1, BLOCKS), block_slot, rcv_cell, observed.reshape(S, CELLS), coupling, log_sigma, sources.reshape(S, BLOCKS, CELLS)
     )
-    return low + high
 
 
 def solution(mesh):

time: 50.1 us -> 46.1 us (0.920)
  Pallas kernels: 48.5 us -> 45.3 us
  other arithmetic: 1.4 us -> 0 us
  local copies, waits for them, and re-layouts: 0 us -> 0.62 us
    pallas_call x1, Pallas kernels: 48.5 us -> 45.3 us  [local(): pl.pallas_call(functools.partial(kernel, ng, nm), out_shape=pltpu.VMEM((O...]
    add x1 -> x0, other arithmetic: 1.4 us -> none  [local(): return low + high]
    unnamed x0 -> x1, local copies, waits for them, and re-layouts: none -> 0.62 us
where the time goes in v4:
time: 46.1 us; the launch traced here: 46 us
  Pallas kernels  45.3 us (98%)
  local copies, waits for them, and re-layouts  0.62 us (1%)
    pallas_call x1, Pallas kernels, local(): pl.pallas_call(functools.partial(kernel, ng, nm), out_shape=pltpu.VMEM((O...  45.3 us

profile of v4, /device:TPU:1, one launch (start us, length us, event | category | flops | bytes accessed | tf_op | source)
XLA Modules:
  0.0 46.0 jit_solution(9919140163894507202)
XLA Ops:
  0.0 45.3 %shard_map.73 = f32[64,128]{1,0:T(8,128)S(1)} custom-call(s32[1,128]{1,0:T(1,128)} %bitcast.5, s32[1,128]{1,0:T(1,128)} %slot_ref.1, s32[1,128]{1,0:T(1,128)} %rcv_ref.1, f32[8,128]{1,0:T(8,128)} %bitcast.4, f32[128,128]{1,0:T(8,128)} %cpl_ref.1, f32[64,128]{1,0:T(8,128)} %ls_ref.1, f32[8,128,128]{2,1,0:T(8,128)} %bitcast.3), custom_call_target="tpu_custom_call" | custom-call | tf_op jit(solution)/shard_map/pallas_call | solution.py:477
  45.3 0.6 %copy.9 = f32[64,128]{1,0:T(8,128)} copy(f32[64,128]{1,0:T(8,128)S(1)} %shard_map.73) | data formatting | bytes 65536

commit v5 on v4

--- a/solution.py
+++ b/solution.py
@@ -18,7 +18,7 @@
 ROWS = HALF * 8
 STAGE = BLOCKS + 2 * HALO
 OWNED = 64
-GROUP = 9
+GROUPS = ((0, 3), (3, 6), (6, 9))
 OMEGA = 0.8
 CHAIN = 1.0
 
@@ -150,6 +150,11 @@
     for z in far_z[::-1]:
         remote(ls_ref.at[own_half, :], table_rows(me), ag_send.at[0], ag_recv.at[mz], m=z_at[z] + mx).start()
 
+    for x in far_x:
+        remote(
+            ls_ref.at[own_half, :], table_rows(me), fan_send.at[0], fan_recv.at[0], m=z_at[0] + x_at[x]
+        ).start()
+
     for side, m in ((0, right), (1, left)):
         for k, ref in enumerate((own_ref, slot_ref, rcv_ref)):
             remote(ref, near.at[side, k], small_send.at[0], small_recv.at[0], m=m).start()
@@ -199,17 +204,29 @@
     slot_of = jnp.sum(pick * (slot_row + 1).astype(f32), axis=1, keepdims=True)
     slots[...] = jnp.broadcast_to(slot_of, (nm * CAP, CELLS)).reshape(nm, CAP, CELLS)
 
-    own_table.wait()
-    for z in [0] + far_z[::-1]:
+    def relay(owner, k, m):
+        remote(table_rows(owner), table_rows(owner), fan_send.at[0], fan_recv.at[k], m=m).start()
+
+    def along_z(z):
         owner = z_at[z] + mx
-        if z:
-            remote(
-                table_rows(owner), table_rows(owner), ag_send.at[0], ag_recv.at[lax.div(z_at[z], NX)], c=other
-            ).wait_recv()
+        remote(
+            table_rows(owner), table_rows(owner), ag_send.at[0], ag_recv.at[lax.div(z_at[z], NX)], c=other
+        ).wait_recv()
+        return owner
+
+    near_z = far_z[1:][::-1]
+    for z in near_z[:2]:
+        owner = along_z(z)
         for x in far_x:
-            remote(
-                table_rows(owner), table_rows(owner), fan_send.at[0], fan_recv.at[0], m=z_at[0] + x_at[x]
-            ).start()
+            relay(owner, 1, z_at[0] + x_at[x])
+    bytes_of(table.at[0:(NX - 1) * half_rows, :], fan_send.at[0], fan_recv.at[0]).wait_recv()
+    for x in far_x[::-1]:
+        relay(z_at[0] + x_at[x], 1, z_at[far_z[0]] + mx)
+    for z in near_z[2:]:
+        owner = along_z(z)
+        for x in far_x:
+            relay(owner, 1, z_at[0] + x_at[x])
+    along_z(far_z[0])
 
     bytes_of(near, small_send.at[0], small_recv.at[0]).wait_recv()
     own3 = jnp.concatenate([near[0, 0], owner_row, near[1, 0]] + [owner_row] * 5, axis=0)
@@ -311,7 +328,8 @@
 
     seams(fwd_a)
 
-    bytes_of(table.at[0:nz * (NX - 1) * half_rows, :], fan_send.at[0], fan_recv.at[0]).wait_recv()
+    own_table.wait()
+    bytes_of(table.at[0:(nz - 1) * (NX - 1) * half_rows, :], fan_send.at[0], fan_recv.at[1]).wait_recv()
     to_scalars.wait()
 
     def pick_rows(first, source, lane):
@@ -348,19 +366,20 @@
     low_lane = iota((64, CELLS), 1) < CELLS // 4
 
     def sweep(old, new, qk, sign, weights):
-        for first in range(0, HALF // 8, GROUP):
-            rows = slice(128 * first, 128 * (first + GROUP))
+        for first, until in GROUPS:
+            rows = slice(128 * first, 128 * until)
             prod = dot(jnp.concatenate([lhs_hi[rows, :], lhs_lo[rows, :]], axis=1), weights[...])
             prod = prod[:, 0:CELLS] + prod[:, CELLS:]
-            for i in range(first, first + GROUP):
+            for i in range(first, until):
                 turn = cross[at64(i), :]
                 near_x = [old[p, 64 * i:64 * i + 80, :] for p in range(2)]
                 for p in range(2):
                     k = 2 * (i - first) + p
                     end = jnp.where(low_lane, near_x[p][16:80], near_x[p][0:64])
                     both = turn * near_x[1 - p][8:72]
-                    x = q[qk, p, at64(i), :] + prod[64 * k:64 * k + 64, :] + ends * pltpu.roll(end, CELLS // 2, axis=1)
+                    x = q[qk, p, at64(i), :] + ends * pltpu.roll(end, CELLS // 2, axis=1)
                     x = x + both if (sign > 0) == (p == 0) else x - both
+                    x = x + prod[64 * k:64 * k + 64, :]
                     put(new, p, i, kept(i, x))
         seams(new)
 
@@ -522,7 +541,7 @@
             dma((1,)), dma((1,)),
             dma((1,)), dma((1,)),
             dma((1,)), dma((nz,)),
-            dma((1,)), dma((1,)),
+            dma((1,)), dma((2,)),
             dma((1,)), dma((1,)),
             dma((1,)), dma((1,)),
             dma((2,)), dma((1,)),

time: 46.1 us -> 45.7 us (level)
  no operation moved by 1% of the time
where the time goes in v5:
time: 45.7 us; the launch traced here: 45.6 us
  Pallas kernels  45 us (98%)
  local copies, waits for them, and re-layouts  0.62 us (1%)
    pallas_call x1, Pallas kernels, local(): pl.pallas_call(functools.partial(kernel, ng, nm), out_shape=pltpu.VMEM((O...  45 us

profile of v5, /device:TPU:1, one launch (start us, length us, event | category | flops | bytes accessed | tf_op | source)
XLA Modules:
  0.0 45.6 jit_solution(14662170146863874760)
XLA Ops:
  0.0 45.0 %shard_map.73 = f32[64,128]{1,0:T(8,128)S(1)} custom-call(s32[1,128]{1,0:T(1,128)} %bitcast.5, s32[1,128]{1,0:T(1,128)} %slot_ref.1, s32[1,128]{1,0:T(1,128)} %rcv_ref.1, f32[8,128]{1,0:T(8,128)} %bitcast.4, f32[128,128]{1,0:T(8,128)} %cpl_ref.1, f32[64,128]{1,0:T(8,128)} %ls_ref.1, f32[8,128,128]{2,1,0:T(8,128)} %bitcast.3), custom_call_target="tpu_custom_call" | custom-call | tf_op jit(solution)/shard_map/pallas_call | solution.py:496
  45.0 0.6 %copy.9 = f32[64,128]{1,0:T(8,128)} copy(f32[64,128]{1,0:T(8,128)S(1)} %shard_map.73) | data formatting | bytes 65536

commit v6 on v5

--- a/solution.py
+++ b/solution.py
@@ -424,11 +424,11 @@
     packed = dot(sel, hi) + dot(sel, mid) + dot(sel, lo)
     pack[...] = packed.reshape(nm, CAP, CELLS)
 
-    takes = lax.rem(mx, 2) == core
+    takes = lax.rem(mx + 1, 2) == core
     for z, x in far:
         m = z_at[z] + x_at[x]
         remote(
-            pack.at[m], pack_in.at[core * nm + me], gp_send.at[0], gp_recv.at[0], m=m, c=lax.rem(x_at[x], 2)
+            pack.at[m], pack_in.at[core * nm + me], gp_send.at[0], gp_recv.at[0], m=m, c=lax.rem(x_at[x] + 1, 2)
         ).start()
     beside_me = remote(pack.at[me], pack_in.at[core * nm + me], gp_send.at[1], gp_recv.at[0], c=other)
 

time: 45.7 us -> 44.3 us (0.969)
  Pallas kernels: 45 us -> 43.5 us
    pallas_call x1, Pallas kernels: 45 us -> 43.5 us  [local(): pl.pallas_call(functools.partial(kernel, ng, nm), out_shape=pltpu.VMEM((O...]
where the time goes in v6:
time: 44.3 us; the launch traced here: 44.2 us
  Pallas kernels  43.5 us (98%)
  local copies, waits for them, and re-layouts  0.62 us (1%)
    pallas_call x1, Pallas kernels, local(): pl.pallas_call(functools.partial(kernel, ng, nm), out_shape=pltpu.VMEM((O...  43.5 us

profile of v6, /device:TPU:1, one launch (start us, length us, event | category | flops | bytes accessed | tf_op | source)
XLA Modules:
  0.0 44.2 jit_solution(17598965828274262033)
XLA Ops:
  0.0 43.5 %shard_map.73 = f32[64,128]{1,0:T(8,128)S(1)} custom-call(s32[1,128]{1,0:T(1,128)} %bitcast.5, s32[1,128]{1,0:T(1,128)} %slot_ref.1, s32[1,128]{1,0:T(1,128)} %rcv_ref.1, f32[8,128]{1,0:T(8,128)} %bitcast.4, f32[128,128]{1,0:T(8,128)} %cpl_ref.1, f32[64,128]{1,0:T(8,128)} %ls_ref.1, f32[8,128,128]{2,1,0:T(8,128)} %bitcast.3), custom_call_target="tpu_custom_call" | custom-call | tf_op jit(solution)/shard_map/pallas_call | solution.py:496
  43.5 0.6 %copy.9 = f32[64,128]{1,0:T(8,128)} copy(f32[64,128]{1,0:T(8,128)S(1)} %shard_map.73) | data formatting | bytes 65536

commit v7 on v6

--- a/solution.py
+++ b/solution.py
@@ -337,19 +337,22 @@
             [table[pl.ds(index_s[source, lane + j], 1), :] for j in range(8)], axis=0
         )
 
-    pick_rows(0, 0, BLOCKS - HALO)
-    pick_rows(HALO + BLOCKS, 2, 0)
-
-    for i in range(BLOCKS // 8):
-        pick_rows(HALO + 8 * i, 1, 8 * i)
-
-    swap = remote(picked, theirs, pick_send.at[0], pick_recv.at[0], c=other)
-    swap.start()
+    def swap_part(k):
+        rows = pl.ds(k * (STAGE // 2), STAGE // 2)
+        return remote(picked.at[rows, :], theirs.at[rows, :], pick_send.at[0], pick_recv.at[0], c=other)
+
+    for i in range(STAGE // 8):
+        source = 0 if i == 0 else 2 if i == STAGE // 8 - 1 else 1
+        pick_rows(8 * i, source, (BLOCKS - HALO, 8 * i - HALO, 0)[source])
+        if i == STAGE // 16 - 1:
+            swap_part(0).start()
+    swap_part(1).start()
 
     for z, x in far:
         m = z_at[z] + x_at[x]
         remote(slots.at[m], slots_in.at[me], sl_send.at[0], sl_recv.at[0], m=m).start()
 
+    swap = bytes_of(picked, pick_send.at[0], pick_recv.at[0])
     swap.wait_recv()
     wsig[...] = OMEGA * jnp.exp(reorder(jnp.where(choose[...] > 0.5, picked[...], theirs[...])))
 
@@ -421,7 +424,7 @@
 
     hi, mid, lo = three(reorder(part[...]))
     sel = qmat[...]
-    packed = dot(sel, hi) + dot(sel, mid) + dot(sel, lo)
+    packed = dot(jnp.concatenate([sel, sel], axis=1), jnp.concatenate([hi, mid], axis=0)) + dot(sel, lo)
     pack[...] = packed.reshape(nm, CAP, CELLS)
 
     takes = lax.rem(mx + 1, 2) == core
@@ -465,7 +468,7 @@
         rows = (pack_in[0:nm] + pack_in[nm:2 * nm]).reshape(nm * CAP, CELLS)
         hi, mid, lo = three(rows)
         sel = hits[0:OWNED, :]
-        line[grp] = dot(sel, hi) + dot(sel, mid) + dot(sel, lo)
+        line[grp] = dot(jnp.concatenate([sel, sel], axis=1), jnp.concatenate([hi, mid], axis=0)) + dot(sel, lo)
 
         for d in far_g:
             remote(line.at[grp], line.at[grp], ln_send.at[0], ln_recv.at[0], g=g_at[d]).start()

time: 44.3 us -> 44.3 us (level)
  no operation moved by 1% of the time
where the time goes in v7:
time: 44.3 us; the launch traced here: 44.1 us
  Pallas kernels  43.5 us (98%)
  local copies, waits for them, and re-layouts  0.62 us (1%)
    pallas_call x1, Pallas kernels, local(): pl.pallas_call(functools.partial(kernel, ng, nm), out_shape=pltpu.VMEM((O...  43.5 us

profile of v7, /device:TPU:1, one launch (start us, length us, event | category | flops | bytes accessed | tf_op | source)
XLA Modules:
  0.0 44.1 jit_solution(3695443067101135538)
XLA Ops:
  0.0 43.5 %shard_map.73 = f32[64,128]{1,0:T(8,128)S(1)} custom-call(s32[1,128]{1,0:T(1,128)} %bitcast.5, s32[1,128]{1,0:T(1,128)} %slot_ref.1, s32[1,128]{1,0:T(1,128)} %rcv_ref.1, f32[8,128]{1,0:T(8,128)} %bitcast.4, f32[128,128]{1,0:T(8,128)} %cpl_ref.1, f32[64,128]{1,0:T(8,128)} %ls_ref.1, f32[8,128,128]{2,1,0:T(8,128)} %bitcast.3), custom_call_target="tpu_custom_call" | custom-call | tf_op jit(solution)/shard_map/pallas_call | solution.py:499
  43.5 0.6 %copy.9 = f32[64,128]{1,0:T(8,128)} copy(f32[64,128]{1,0:T(8,128)S(1)} %shard_map.73) | data formatting | bytes 65536
